TPU v7x, 32 devices: a whole 2x2x4 slice. The times are simulated.
32 devices in a mesh: fsdp: 4 (over y, x), seq: 8 (over z, core).
Axes of the slice: x: 2, y: 2, z: 4, core: 2. Of those that a mesh axis runs over, the one named last changes fastest.
Arguments:
- q_next: bfloat16 [4096, 4096], P(('fsdp', 'seq')), may hold values from -9 to 9
- k_next: bfloat16 [4096, 1024], P(('fsdp', 'seq')), may hold values from -4 to 4
- v_next: bfloat16 [4096, 1024], P(('fsdp', 'seq')), may hold values from -6 to 6
- seg_next: int32 [4, 1024], P('fsdp'), may hold values from 0 to 3, never falling along the last dimension, each value on 1 to 512 neighbouring positions
- q_prev: bfloat16 [4096, 4096], P(('fsdp', 'seq')), may hold values from -9 to 9
- k_prev: bfloat16 [4096, 1024], P(('fsdp', 'seq')), may hold values from -4 to 4
- v_prev: bfloat16 [4096, 1024], P(('fsdp', 'seq')), may hold values from -6 to 6
- seg_prev: int32 [4, 1024], P('fsdp'), may hold values from 0 to 3, never falling along the last dimension, each value on 1 to 512 neighbouring positions
- upstream: bfloat16 [4096, 4096], P(('fsdp', 'seq')), may hold values from -6 to 6
- flags: int32 [4, 1024], P('fsdp', 'seq'), may hold values from 0 to 1
Outputs:
- attn_next: bfloat16 [4096, 4096], P(('fsdp', 'seq'))
- grad_q: bfloat16 [4096, 4096], P(('fsdp', 'seq'))
- grad_k: bfloat16 [4096, 1024], P(('fsdp', 'seq'))
- grad_v: bfloat16 [4096, 1024], P(('fsdp', 'seq'))
Inputs may be any that keep to these rules, and one draw needn't show every extreme that they name: `seg_next`: within each sequence the ids never fall and each id covers at most 512 consecutive positions; some id covers exactly 512. `seg_prev`: within each sequence the ids never fall and each id covers at most 512 consecutive positions; some id covers exactly 512.
All inputs are finite; a program needn't handle non-finite values.
Results may differ from a plain program's by a relative error of at most 0.0067.
Values may be sent and summed in bfloat16 or wider, within the bound.
A program may use at most 128 MiB of HBM per device.

v0:
```python
import jax
import jax.numpy as jnp
from jax import lax
from jax.sharding import PartitionSpec as P

HEAD_DIM = 128


def passed_along(block, axis, distance):
    devices = range(lax.axis_size(axis))
    route = [(i - distance, i) for i in devices if i - distance in devices]
    return lax.ppermute(block, axis, route)


def masked_probs(q_block, k_window, q_pos, k_pos, q_seg, k_seg, scale_factor):
    scores = (
        jnp.einsum("qhd,khd->hqk", q_block, k_window, preferred_element_type=jnp.float32)
        * scale_factor
    )
    keep_mask = (k_seg[None, :] == q_seg[:, None]) & (k_pos[None, :] <= q_pos[:, None])
    scores = jnp.where(keep_mask[None], scores, -1e30)
    row_max = jnp.max(scores, axis=-1, keepdims=True)
    expo_vals = jnp.exp(scores - row_max)
    return expo_vals / jnp.sum(expo_vals, axis=-1, keepdims=True)


def block_window(seq_ids, block_start, block_len, reach):
    padded = jnp.concatenate([jnp.full((reach,), -1, jnp.int32), seq_ids])
    q_seg = lax.dynamic_slice_in_dim(seq_ids, block_start, block_len)
    k_seg = lax.dynamic_slice_in_dim(padded, block_start, reach + block_len)
    q_pos = block_start + jnp.arange(block_len, dtype=jnp.int32)
    k_pos = block_start - reach + jnp.arange(reach + block_len, dtype=jnp.int32)
    return (q_pos, k_pos, q_seg, k_seg)


def pad_front(array, reach):
    return jnp.concatenate([jnp.zeros((reach,) + array.shape[1:], array.dtype), array], axis=0)


def forward_heads(q_heads, k_heads, v_heads, seq_ids, reach, block_len, scale_factor):
    seq_len = q_heads.shape[0]
    k_padded = pad_front(k_heads, reach)
    v_padded = pad_front(v_heads, reach)

    def block_step(block_idx, output):
        block_start = (block_idx * block_len).astype(jnp.int32)
        q_pos, k_pos, q_seg, k_seg = block_window(seq_ids, block_start, block_len, reach)
        q_block = lax.dynamic_slice_in_dim(q_heads, block_start, block_len, 0)
        k_window = lax.dynamic_slice_in_dim(k_padded, block_start, reach + block_len, 0)
        v_window = lax.dynamic_slice_in_dim(v_padded, block_start, reach + block_len, 0)
        soft_probs = masked_probs(q_block, k_window, q_pos, k_pos, q_seg, k_seg, scale_factor)
        result = jnp.einsum(
            "hqk,khd->qhd",
            soft_probs.astype(jnp.bfloat16),
            v_window,
            preferred_element_type=jnp.float32,
        )
        return lax.dynamic_update_slice_in_dim(output, result.astype(jnp.bfloat16), block_start, 0)

    return lax.fori_loop(
        0, seq_len // block_len, block_step, jnp.zeros(q_heads.shape, jnp.bfloat16)
    )


def window_meta(seq_ids, rows_here, hop_total):
    width_all = (hop_total + 1) * rows_here
    first_row = lax.axis_index("seq") * rows_here
    padded = jnp.concatenate([jnp.full((hop_total * rows_here,), -1, jnp.int32), seq_ids])
    k_seg = lax.dynamic_slice_in_dim(padded, first_row, width_all)
    q_seg = lax.dynamic_slice_in_dim(seq_ids, first_row, rows_here)
    q_pos = first_row + jnp.arange(rows_here, dtype=jnp.int32)
    k_pos = first_row - hop_total * rows_here + jnp.arange(width_all, dtype=jnp.int32)
    keep_mask = (k_seg[None, :] == q_seg[:, None]) & (k_pos[None, :] <= q_pos[:, None])
    return keep_mask


def grouped_probs(grouped, k_window, keep_mask, scale_factor):
    scores = (
        jnp.einsum("qjgd,kjd->jgqk", grouped, k_window, preferred_element_type=jnp.float32)
        * scale_factor
    )
    scores = jnp.where(keep_mask[None, None], scores, -1e30)
    row_max = jnp.max(scores, axis=-1, keepdims=True)
    expo_vals = jnp.exp(scores - row_max)
    return expo_vals / jnp.sum(expo_vals, axis=-1, keepdims=True)


def backward_local(q_local, k_local, v_local, d_local, seq_ids, reach, scale_factor):
    rows_here = q_local.shape[0]
    head_dim = HEAD_DIM
    heads_all = q_local.shape[1] // head_dim
    kv_heads = k_local.shape[1] // head_dim
    group_size = heads_all // kv_heads
    hop_total = (reach + rows_here - 1) // rows_here
    key_list = [k_local]
    value_list = [v_local]
    for hop_count in range(1, hop_total + 1):
        far_keys, far_values = passed_along((k_local, v_local), "seq", hop_count)
        key_list.insert(0, far_keys)
        value_list.insert(0, far_values)
    width_all = (hop_total + 1) * rows_here
    k_window = jnp.concatenate(key_list, axis=0).reshape(width_all, kv_heads, head_dim)
    v_window = jnp.concatenate(value_list, axis=0).reshape(width_all, kv_heads, head_dim)
    keep_mask = window_meta(seq_ids, rows_here, hop_total)
    grouped_q = q_local.reshape(rows_here, kv_heads, group_size, head_dim)
    grouped_d = d_local.reshape(rows_here, kv_heads, group_size, head_dim)
    soft_probs = grouped_probs(grouped_q, k_window, keep_mask, scale_factor)
    d_probs = jnp.einsum("qjgd,kjd->jgqk", grouped_d, v_window, preferred_element_type=jnp.float32)
    row_delta = jnp.sum(soft_probs * d_probs, axis=-1, keepdims=True)
    d_scores = (soft_probs * (d_probs - row_delta) * scale_factor).astype(jnp.bfloat16)
    q_grad = jnp.einsum("jgqk,kjd->qjgd", d_scores, k_window, preferred_element_type=jnp.float32)
    q_grad = q_grad.astype(jnp.bfloat16).reshape(rows_here, heads_all * head_dim)
    k_term = jnp.einsum(
        "jgqk,qjgd->kjd", d_scores, grouped_q, preferred_element_type=jnp.float32
    ).reshape(width_all, kv_heads * head_dim)
    v_term = jnp.einsum(
        "jgqk,qjgd->kjd",
        soft_probs.astype(jnp.bfloat16),
        grouped_d,
        preferred_element_type=jnp.float32,
    ).reshape(width_all, kv_heads * head_dim)
    k_total = k_term[hop_total * rows_here :]
    v_total = v_term[hop_total * rows_here :]
    for hop_count in range(1, hop_total + 1):
        start_row = (hop_total - hop_count) * rows_here
        back_keys, back_values = passed_along(
            (k_term[start_row : start_row + rows_here], v_term[start_row : start_row + rows_here]),
            "seq",
            -hop_count,
        )
        k_total = k_total + back_keys
        v_total = v_total + back_values
    return (q_grad, k_total.astype(jnp.bfloat16), v_total.astype(jnp.bfloat16))


def body(q_next, k_next, v_next, seg_next, q_prev, k_prev, v_prev, seg_prev, upstream, flags):
    rows_here = q_next.shape[0]
    head_dim = HEAD_DIM
    heads_all = q_next.shape[1] // head_dim
    kv_heads = k_next.shape[1] // head_dim
    group_size = heads_all // kv_heads
    seq_size = lax.axis_size("seq")
    seq_len = rows_here * seq_size
    token_total = rows_here * lax.axis_size("fsdp") * seq_size
    reach = min(512, 4 * rows_here, seq_len // 2)
    block_len = min(512, seq_len)
    scale_factor = head_dim ** (-0.5)
    heads_here = heads_all // seq_size
    next_ids = seg_next[0]
    prev_ids = seg_prev[0]
    flag_total = lax.psum(jnp.sum(flags.astype(jnp.float32)), ("fsdp", "seq"))
    weight = flags.reshape(rows_here, 1).astype(jnp.float32) * (
        token_total / jnp.maximum(flag_total, 1.0)
    )
    cotangent = (upstream.astype(jnp.float32) * weight).astype(jnp.bfloat16)

    def shared_heads(array):
        split_heads = array.reshape(rows_here, kv_heads, head_dim)
        return jnp.repeat(split_heads, group_size, axis=1).reshape(rows_here, heads_all * head_dim)

    def as_heads(array):
        return array.reshape(seq_len, heads_here, head_dim)

    next_in = (
        lax.all_to_all(q_next, "seq", split_axis=1, concat_axis=0, tiled=True),
        lax.all_to_all(shared_heads(k_next), "seq", split_axis=1, concat_axis=0, tiled=True),
        lax.all_to_all(shared_heads(v_next), "seq", split_axis=1, concat_axis=0, tiled=True),
    )
    out_heads = forward_heads(
        as_heads(next_in[0]),
        as_heads(next_in[1]),
        as_heads(next_in[2]),
        next_ids,
        reach,
        block_len,
        scale_factor,
    )
    attn_next = lax.all_to_all(
        out_heads.reshape(seq_len, heads_here * head_dim),
        "seq",
        split_axis=0,
        concat_axis=1,
        tiled=True,
    )
    grad_q, grad_k, grad_v = backward_local(
        q_prev, k_prev, v_prev, cotangent, prev_ids, reach, scale_factor
    )
    return (attn_next, grad_q, grad_k, grad_v)


def solution(mesh):
    return jax.shard_map(
        body,
        mesh=mesh,
        in_specs=(
            P(("fsdp", "seq"), None),
            P(("fsdp", "seq"), None),
            P(("fsdp", "seq"), None),
            P("fsdp", None),
            P(("fsdp", "seq"), None),
            P(("fsdp", "seq"), None),
            P(("fsdp", "seq"), None),
            P("fsdp", None),
            P(("fsdp", "seq"), None),
            P("fsdp", "seq"),
        ),
        out_specs=(
            P(("fsdp", "seq"), None),
            P(("fsdp", "seq"), None),
            P(("fsdp", "seq"), None),
            P(("fsdp", "seq"), None),
        ),
        check_vma=False,
    )
```

profile of v0, /device:TPU:22, one launch (start us, length us, event | category | flops | bytes accessed | tf_op | source)
XLA Modules:
  0.0 331.5 jit_solution(18408808824649141956)
XLA Ops:
  0.6 1.2 copy.158
  1.9 1.2 broadcast_in_dim.84
  3.1 5.2 %all-to-all-start = ((bf16[128,8,512]{0,2,1:T(8,128)(2,1)}), bf16[128,8,512]{0,2,1:T(8,128)(2,1)S(1)}, u32[]{:S(2)}, u32[]{:S(2)}) async-start(bf16[128,8,512]{0,2,1:T(8,128)(2,1)} %bitcast.2), calls=%async_computation | async-start | bytes 2097152 | tf_op jit(solution)/shard_map/all_to_all | solution.py:167
  8.3 1.8 copy.126
  10.1 2.0 collective-permute-start.7
  12.1 3.4 %collective-permute-start.6 = (bf16[128,1024]{0,1:T(8,128)(2,1)}, bf16[128,1024]{0,1:T(8,128)(2,1)}, u32[]{:S(2)}, u32[]{:S(2)}) collective-permute-start(bf16[128,1024]{0,1:T(8,128)(2,1)} %copy.126), channel_id=1, source_target_pairs={{0,2},{1,3},{2,4},{3,5},{4,6},{5,7},{8,10},{9,11},{10,12},{11,13},... | collective-permute-start | bytes 786440 | tf_op jit(solution)/shard_map/ppermute | solution.py:12
  15.5 1.1 copy.119
  16.6 1.9 collective-permute-start.2
  18.5 1.9 collective-permute-start.1
  20.5 1.3 convert_reduce_fusion
  21.7 1.3 collective-permute-start
  23.0 60.0 %psum.7 = f32[]{:T(128)} all-reduce(f32[]{:T(128)} %convert_reduce_fusion), channel_id=1, replica_groups=mesh['fsdp'=4,'seq'=8] {'fsdp','seq'}, use_global_device_ids=true, to_apply=%region_7.8 | all-reduce | flops 1 | bytes 8 | tf_op jit(solution)/shard_map/psum | solution.py:151
  83.0 1.1 copy.159
  86.3 1.2 broadcast_in_dim.85
  87.5 7.1 %all-to-all-start.2 = ((bf16[128,8,512]{0,2,1:T(8,128)(2,1)}), bf16[128,8,512]{0,2,1:T(8,128)(2,1)}, u32[]{:S(2)}, u32[]{:S(2)}) async-start(bf16[128,8,512]{0,2,1:T(8,128)(2,1)} %bitcast.8), calls=%async_computation.2 | async-start | bytes 2097152 | tf_op jit(solution)/shard_map/all_to_all | solution.py:166
  96.5 2.6 copy.111
  99.2 2.3 copy.167
  101.4 2.0 collective-permute-start.3
  104.5 2.4 collective-permute-start.5
  107.9 1.3 collective-permute-start.4
  110.2 22.5 %collective-permute-done.3 = bf16[128,1024]{0,1:T(8,128)(2,1)S(1)} collective-permute-done((bf16[128,1024]{0,1:T(8,128)(2,1)S(1)}, bf16[128,1024]{0,1:T(8,128)(2,1)S(1)}, u32[]{:S(2)}, u32[]{:S(2)}) %collective-permute-start.3) | collective-permute-done | bytes 262176 | tf_op jit(solution)/shard_map/ppermute | solution.py:12
  135.0 12.0 %all-to-all-start.1 = ((bf16[128,8,512]{0,2,1:T(8,128)(2,1)}), bf16[128,8,512]{0,2,1:T(8,128)(2,1)}, u32[]{:S(2)}, u32[]{:S(2)}) async-start(bf16[128,8,512]{0,2,1:T(8,128)(2,1)} %bitcast.5), calls=%async_computation.1 | async-start | bytes 2097152 | tf_op jit(solution)/shard_map/all_to_all | solution.py:165
  149.0 5.5 %fusion.48 = f32[8,640,128,4]{2,1,3,0:T(8,128)} fusion(bf16[640,8,128,1]{0,2,3,1:T(8,128)(2,1)S(1)} %bitcast.138, bf16[128,8,4,128]{0,3,2,1:T(8,128)(2,1)S(1)} %bitcast.122), kind=kOutput, calls=%fused_computation.77 | convolution fusion | flops 671088640 | bytes 12845056 | tf_op jit(solution)/shard_map/qjgd,kjd->jgqk/dot_general | solution.py:108
  154.5 9.1 %fusion.47 = (f32[8,4,128]{2,1,0:T(4,128)S(1)}, f32[8,4,128,640]{2,3,1,0:T(8,128)}) fusion(pred[128,640]{0,1:T(8,128)(4,1)S(1)} %compare_and_fusion.1, bf16[640,8,128,1]{0,2,3,1:T(8,128)(2,1)} %bitcast.145, bf16[128,8,4,128]{0,3,2,1:T(8,128)(2,1)} %bitcast.141), kind=kOutput, calls=%fused_computation.76 | convolution fusion | flops 681575040 | bytes 12943360 | tf_op jit(solution)/shard_map/sub | solution.py:84
  163.6 16.4 %fusion.34 = f32[640,8,128]{0,2,1:T(8,128)} fusion(bf16[128,8,4,128]{0,3,2,1:T(8,128)(2,1)S(1)} %bitcast.142, f32[8,640,128,4]{2,1,3,0:T(8,128)} %fusion.48, f32[8,4,128,640]{2,3,1,0:T(8,128)} %get-tuple-element.220, f32[8,4,128]{2,1,0:T(4,128)S(1)} %get-tuple-element.219), kind=kOutput, calls=%fused_computation.45 | convolution fusion | flops 689443456 | bytes 24657920 | tf_op jit(solution)/shard_map/jgqk,qjgd->kjd/dot_general | solution.py:113
  180.0 2.7 fusion.46
  183.7 1.0 copy.139
  185.7 2.5 collective-permute-start.9
  188.2 1.9 collective-permute-start.10
  190.1 2.3 collective-permute-start.11
  193.6 2.9 copy.114
  196.5 1.5 reshape.227
  198.0 1.3 concatenate.20
  199.5 2.9 copy.112
  202.3 1.5 reshape.225
  203.9 1.1 broadcast_in_dim.83
  205.0 27.9 %while.15 = (s32[]{:T(128)}, bf16[1024,4,128]{0,2,1:T(8,128)(2,1)}, bf16[1536,4,128]{0,2,1:T(8,128)(2,1)}, s32[1024]{0:T(1024)S(1)}, bf16[1024,4,128]{0,2,1:T(8,...) while((s32[]{:T(128)}, bf16[1024,4,128]{0,2,1:T(8,128)(2,1)}, ...), condition=%wide.region_3.0_spmd, body=%wide.region_0.3_spmd.sunk | while | flops 1092356608 | bytes 52476220 | solution.py:60
  205.6 1.3 fusion.67
  206.9 6.0 %fusion.68 = (f32[4,512]{1,0:T(4,128)S(1)}, f32[4,512,1024]{2,1,0:T(8,128)}) fusion(f32[4,512,1024]{2,1,0:T(8,128)S(1)} %fusion.67, pred[512,1024]{1,0:T(8,128)(4,1)S(1)} %compare_and_fusion.3), kind=kOutput, calls=%fused_computation.73.clone.1 | output fusion | flops 12583935 | bytes 17309696 | tf_op jit(solution)/shard_map/while/body/eval_jaxpr/sub | solution.py:23
  212.9 5.0 %fusion.69 = bf16[1024,4,128]{0,2,1:T(8,128)(2,1)S(1)} fusion(bf16[1024,4,128]{0,2,1:T(8,128)(2,1)S(1)} %copy-done.1, s32[]{:T(128)S(6)} %select_n.72, f32[4,512,1024]{2,1,0:T(8,128)} %get-tuple-element.266, f32[4,512]{1,0:T(4,128)S(1)} %get-tuple-element.267, bf16[1536,4,128]{0,2,1:T(8,128)(2,1)S(1)} %copy-done.4, s32[]{:T(128)S(6)} %select_n.73), kind=kOutput, calls=%fused_computation.12.clone.1 | convolution fusion | flops 541327360 | bytes 9969672 | tf_op jit(solution)/shard_map/while/body/eval_jaxpr/hqk,khd->qhd/dot_general | solution.py:52
  219.6 1.3 fusion.67
  220.9 6.0 %fusion.68 = (f32[4,512]{1,0:T(4,128)S(1)}, f32[4,512,1024]{2,1,0:T(8,128)}) fusion(f32[4,512,1024]{2,1,0:T(8,128)S(1)} %fusion.67, pred[512,1024]{1,0:T(8,128)(4,1)S(1)} %compare_and_fusion.3), kind=kOutput, calls=%fused_computation.73.clone.1 | output fusion | flops 12583935 | bytes 17309696 | tf_op jit(solution)/shard_map/while/body/eval_jaxpr/sub | solution.py:23
  226.9 5.0 %fusion.69 = bf16[1024,4,128]{0,2,1:T(8,128)(2,1)S(1)} fusion(bf16[1024,4,128]{0,2,1:T(8,128)(2,1)S(1)} %copy-done.1, s32[]{:T(128)S(6)} %select_n.72, f32[4,512,1024]{2,1,0:T(8,128)} %get-tuple-element.266, f32[4,512]{1,0:T(4,128)S(1)} %get-tuple-element.267, bf16[1536,4,128]{0,2,1:T(8,128)(2,1)S(1)} %copy-done.4, s32[]{:T(128)S(6)} %select_n.73), kind=kOutput, calls=%fused_computation.12.clone.1 | convolution fusion | flops 541327360 | bytes 9969672 | tf_op jit(solution)/shard_map/while/body/eval_jaxpr/hqk,khd->qhd/dot_general | solution.py:52
  232.9 1.5 copy.169
  234.4 1.5 copy.160
  235.8 6.2 %all-to-all-start.3 = ((bf16[8,128,512]{2,1,0:T(8,128)(2,1)}), bf16[8,128,512]{2,1,0:T(8,128)(2,1)S(1)}, u32[]{:S(2)}, u32[]{:S(2)}) async-start(bf16[8,128,512]{2,1,0:T(8,128)(2,1)} %copy.160), calls=%async_computation.3 | async-start | bytes 2097152 | tf_op jit(solution)/shard_map/all_to_all | solution.py:178
  242.0 7.6 %fusion.31 = f32[640,8,128]{0,2,1:T(8,128)} fusion(bf16[128,8,4,128]{0,3,2,1:T(8,128)(2,1)} %bitcast.123, f32[8,4,128,640]{2,3,1,0:T(8,128)} %get-tuple-element.220, f32[8,4,128]{2,1,0:T(4,128)S(1)} %get-tuple-element.219), kind=kOutput, calls=%fused_computation.44 | convolution fusion | flops 676331520 | bytes 14172160 | tf_op jit(solution)/shard_map/jgqk,qjgd->kjd/dot_general | solution.py:116
  250.6 2.2 collective-permute-start.8
  252.8 2.9 fusion.45
  255.7 2.0 copy.143
  257.8 2.0 copy.147
  261.8 2.3 collective-permute-start.13
  264.1 1.9 collective-permute-start.14
  266.1 2.1 collective-permute-start.15
  268.2 2.1 collective-permute-start.12
  270.3 15.3 %fusion.35 = bf16[8,128,4,128]{3,1,2,0:T(8,128)(2,1)S(1)} fusion(bf16[640,8,128,1]{0,2,3,1:T(8,128)(2,1)} %bitcast.146, f32[8,640,128,4]{2,1,3,0:T(8,128)} %fusion.48, f32[8,4,128,640]{2,3,1,0:T(8,128)} %get-tuple-element.220, f32[8,4,128]{2,1,0:T(4,128)S(1)} %get-tuple-element.219), kind=kOutput, calls=%fused_computation.46 | convolution fusion | flops 689967744 | bytes 23347200 | tf_op jit(solution)/shard_map/jgqk,kjd->qjgd/dot_general | solution.py:111
  285.6 1.3 copy.149
  287.3 2.4 add_convert_fusion.1
  289.7 15.4 %collective-permute-done.13 = f32[128,1024]{1,0:T(8,128)} collective-permute-done((f32[128,1024]{1,0:T(8,128)}, f32[128,1024]{1,0:T(8,128)}, u32[]{:S(2)}, u32[]{:S(2)}) %collective-permute-start.13) | collective-permute-done | bytes 524320 | tf_op jit(solution)/shard_map/ppermute | solution.py:12
  305.1 10.8 %collective-permute-done.14 = f32[128,1024]{1,0:T(8,128)} collective-permute-done((f32[128,1024]{1,0:T(8,128)}, f32[128,1024]{1,0:T(8,128)}, u32[]{:S(2)}, u32[]{:S(2)}) %collective-permute-start.14) | collective-permute-done | bytes 524320 | tf_op jit(solution)/shard_map/ppermute | solution.py:12
  315.9 5.6 %collective-permute-done.15 = f32[128,1024]{1,0:T(8,128)} collective-permute-done((f32[128,1024]{1,0:T(8,128)}, f32[128,1024]{1,0:T(8,128)}, u32[]{:S(2)}, u32[]{:S(2)}) %collective-permute-start.15) | collective-permute-done | bytes 524320 | tf_op jit(solution)/shard_map/ppermute | solution.py:12
  321.5 5.6 %collective-permute-done.12 = f32[128,1024]{1,0:T(8,128)} collective-permute-done((f32[128,1024]{1,0:T(8,128)}, f32[128,1024]{1,0:T(8,128)}, u32[]{:S(2)}, u32[]{:S(2)}) %collective-permute-start.12) | collective-permute-done | bytes 524320 | tf_op jit(solution)/shard_map/ppermute | solution.py:12
  327.1 2.4 add_convert_fusion
  330.2 1.3 copy.148
  (75 shorter events, 21.1 us)
Async XLA Ops:
  0.6 94.0 %copy-start.5 = (bf16[128,4096]{1,0:T(8,128)(2,1)S(1)}, bf16[128,4096]{1,0:T(8,128)(2,1)}, u32[]{:S(2)}) copy-start(bf16[128,4096]{1,0:T(8,128)(2,1)} %param.20) | copy-start | bytes 3145732
  3.1 83.2 %all-to-all-start = ((bf16[128,8,512]{0,2,1:T(8,128)(2,1)}), bf16[128,8,512]{0,2,1:T(8,128)(2,1)S(1)}, u32[]{:S(2)}, u32[]{:S(2)}) async-start(bf16[128,8,512]{0,2,1:T(8,128)(2,1)} %bitcast.2), calls=%async_computation | async-start | bytes 2097152 | tf_op jit(solution)/shard_map/all_to_all | solution.py:167
  10.1 136.8 %collective-permute-start.7 = (bf16[128,1024]{0,1:T(8,128)(2,1)}, bf16[128,1024]{0,1:T(8,128)(2,1)}, u32[]{:S(2)}, u32[]{:S(2)}) collective-permute-start(bf16[128,1024]{0,1:T(8,128)(2,1)} %copy.126), channel_id=1, source_target_pairs={{0,1},{1,2},{2,3},{3,4},{4,5},{5,6},{6,7},{8,9},{9,10},{10,11},{11... | collective-permute-start | bytes 786440 | tf_op jit(solution)/shard_map/ppermute | solution.py:12
  12.1 121.8 %collective-permute-start.6 = (bf16[128,1024]{0,1:T(8,128)(2,1)}, bf16[128,1024]{0,1:T(8,128)(2,1)}, u32[]{:S(2)}, u32[]{:S(2)}) collective-permute-start(bf16[128,1024]{0,1:T(8,128)(2,1)} %copy.126), channel_id=1, source_target_pairs={{0,2},{1,3},{2,4},{3,5},{4,6},{5,7},{8,10},{9,11},{10,12},{11,13},... | collective-permute-start | bytes 786440 | tf_op jit(solution)/shard_map/ppermute | solution.py:12
  16.6 91.3 %collective-permute-start.2 = (bf16[128,1024]{0,1:T(8,128)(2,1)S(1)}, bf16[128,1024]{0,1:T(8,128)(2,1)}, u32[]{:S(2)}, u32[]{:S(2)}) collective-permute-start(bf16[128,1024]{0,1:T(8,128)(2,1)S(1)} %copy.119), channel_id=1, source_target_pairs={{0,2},{1,3},{2,4},{3,5},{4,6},{5,7},{8,10},{9,11},{10,12},{11,13},... | collective-permute-start | bytes 786440 | tf_op jit(solution)/shard_map/ppermute | solution.py:12
  18.5 85.9 %collective-permute-start.1 = (bf16[128,1024]{0,1:T(8,128)(2,1)S(1)}, bf16[128,1024]{0,1:T(8,128)(2,1)}, u32[]{:S(2)}, u32[]{:S(2)}) collective-permute-start(bf16[128,1024]{0,1:T(8,128)(2,1)S(1)} %copy.119), channel_id=1, source_target_pairs={{0,3},{1,4},{2,5},{3,6},{4,7},{8,11},{9,12},{10,13},{11,14},{12,15... | collective-permute-start | bytes 786440 | tf_op jit(solution)/shard_map/ppermute | solution.py:12
  21.7 79.7 %collective-permute-start = (bf16[128,1024]{0,1:T(8,128)(2,1)S(1)}, bf16[128,1024]{0,1:T(8,128)(2,1)}, u32[]{:S(2)}, u32[]{:S(2)}) collective-permute-start(bf16[128,1024]{0,1:T(8,128)(2,1)S(1)} %copy.119), channel_id=1, source_target_pairs={{0,4},{1,5},{2,6},{3,7},{8,12},{9,13},{10,14},{11,15},{16,20},{17,... | collective-permute-start | bytes 786440 | tf_op jit(solution)/shard_map/ppermute | solution.py:12
  87.5 47.4 %all-to-all-start.2 = ((bf16[128,8,512]{0,2,1:T(8,128)(2,1)}), bf16[128,8,512]{0,2,1:T(8,128)(2,1)}, u32[]{:S(2)}, u32[]{:S(2)}) async-start(bf16[128,8,512]{0,2,1:T(8,128)(2,1)} %bitcast.8), calls=%async_computation.2 | async-start | bytes 2097152 | tf_op jit(solution)/shard_map/all_to_all | solution.py:166
  96.5 58.0 %copy-start = (bf16[128,4096]{0,1:T(8,128)(2,1)}, bf16[128,4096]{0,1:T(8,128)(2,1)S(1)}, u32[]{:S(2)}) copy-start(bf16[128,4096]{0,1:T(8,128)(2,1)S(1)} %copy.168) | copy-start | bytes 3145732
  101.4 31.3 %collective-permute-start.3 = (bf16[128,1024]{0,1:T(8,128)(2,1)S(1)}, bf16[128,1024]{0,1:T(8,128)(2,1)S(1)}, u32[]{:S(2)}, u32[]{:S(2)}) collective-permute-start(bf16[128,1024]{0,1:T(8,128)(2,1)S(1)} %copy.119), channel_id=1, source_target_pairs={{0,1},{1,2},{2,3},{3,4},{4,5},{5,6},{6,7},{8,9},{9,10},{10,11},{11... | collective-permute-start | bytes 786440 | tf_op jit(solution)/shard_map/ppermute | solution.py:12
  104.5 28.5 %collective-permute-start.5 = (bf16[128,1024]{0,1:T(8,128)(2,1)}, bf16[128,1024]{0,1:T(8,128)(2,1)S(1)}, u32[]{:S(2)}, u32[]{:S(2)}) collective-permute-start(bf16[128,1024]{0,1:T(8,128)(2,1)} %copy.126), channel_id=1, source_target_pairs={{0,3},{1,4},{2,5},{3,6},{4,7},{8,11},{9,12},{10,13},{11,14},{12,15... | collective-permute-start | bytes 786440 | tf_op jit(solution)/shard_map/ppermute | solution.py:12
  107.9 25.0 %collective-permute-start.4 = (bf16[128,1024]{0,1:T(8,128)(2,1)}, bf16[128,1024]{0,1:T(8,128)(2,1)S(1)}, u32[]{:S(2)}, u32[]{:S(2)}) collective-permute-start(bf16[128,1024]{0,1:T(8,128)(2,1)} %copy.126), channel_id=1, source_target_pairs={{0,4},{1,5},{2,6},{3,7},{8,12},{9,13},{10,14},{11,15},{16,20},{17,... | collective-permute-start | bytes 786440 | tf_op jit(solution)/shard_map/ppermute | solution.py:12
  132.9 1.1 copy-start.8
  135.0 64.5 %all-to-all-start.1 = ((bf16[128,8,512]{0,2,1:T(8,128)(2,1)}), bf16[128,8,512]{0,2,1:T(8,128)(2,1)}, u32[]{:S(2)}, u32[]{:S(2)}) async-start(bf16[128,8,512]{0,2,1:T(8,128)(2,1)} %bitcast.5), calls=%async_computation.1 | async-start | bytes 2097152 | tf_op jit(solution)/shard_map/all_to_all | solution.py:165
  154.5 9.1 %copy-start.6 = (bf16[128,4096]{0,1:T(8,128)(2,1)S(1)}, bf16[128,4096]{0,1:T(8,128)(2,1)}, u32[]{:S(2)}) copy-start(bf16[128,4096]{0,1:T(8,128)(2,1)} %copy.167) | copy-start | bytes 3145732
  185.7 78.4 %collective-permute-start.9 = (f32[128,1024]{1,0:T(8,128)}, f32[128,1024]{1,0:T(8,128)}, u32[]{:S(2)}, u32[]{:S(2)}) collective-permute-start(f32[128,1024]{1,0:T(8,128)} %copy.138), channel_id=1, source_target_pairs={{2,0},{3,1},{4,2},{5,3},{6,4},{7,5},{10,8},{11,9},{12,10},{13,11},... | collective-permute-start | bytes 1572872 | tf_op jit(solution)/shard_map/ppermute | solution.py:12
  188.2 77.9 %collective-permute-start.10 = (f32[128,1024]{1,0:T(8,128)}, f32[128,1024]{1,0:T(8,128)}, u32[]{:S(2)}, u32[]{:S(2)}) collective-permute-start(f32[128,1024]{1,0:T(8,128)} %copy.139), channel_id=1, source_target_pairs={{3,0},{4,1},{5,2},{6,3},{7,4},{11,8},{12,9},{13,10},{14,11},{15,12... | collective-permute-start | bytes 1572872 | tf_op jit(solution)/shard_map/ppermute | solution.py:12
  190.1 78.0 %collective-permute-start.11 = (f32[128,1024]{1,0:T(8,128)}, f32[128,1024]{1,0:T(8,128)}, u32[]{:S(2)}, u32[]{:S(2)}) collective-permute-start(f32[128,1024]{1,0:T(8,128)} %copy.140), channel_id=1, source_target_pairs={{4,0},{5,1},{6,2},{7,3},{12,8},{13,9},{14,10},{15,11},{20,16},{21,... | collective-permute-start | bytes 1572872 | tf_op jit(solution)/shard_map/ppermute | solution.py:12
  193.1 11.9 %copy-start.7 = (s32[1,1024]{1,0:T(1,128)S(1)}, s32[1,1024]{1,0:T(1,128)}, u32[]{:S(2)}) copy-start(s32[1,1024]{1,0:T(1,128)} %param.15) | copy-start | bytes 12292
  206.9 6.0 %copy-start.1 = (bf16[1024,4,128]{0,2,1:T(8,128)(2,1)S(1)}, bf16[1024,4,128]{0,2,1:T(8,128)(2,1)}, u32[]{:S(2)}) copy-start(bf16[1024,4,128]{0,2,1:T(8,128)(2,1)} %get-tuple-element.281) | copy-start | bytes 3145732 | tf_op jit(solution)/shard_map/while
  206.9 6.0 %copy-start.4 = (bf16[1536,4,128]{0,2,1:T(8,128)(2,1)S(1)}, bf16[1536,4,128]{0,2,1:T(8,128)(2,1)}, u32[]{:S(2)}) copy-start(bf16[1536,4,128]{0,2,1:T(8,128)(2,1)} %get-tuple-element.294) | copy-start | bytes 4718596 | tf_op jit(solution)/shard_map/while
  217.9 1.0 copy-start.2
  220.9 6.0 %copy-start.1 = (bf16[1024,4,128]{0,2,1:T(8,128)(2,1)S(1)}, bf16[1024,4,128]{0,2,1:T(8,128)(2,1)}, u32[]{:S(2)}) copy-start(bf16[1024,4,128]{0,2,1:T(8,128)(2,1)} %get-tuple-element.281) | copy-start | bytes 3145732 | tf_op jit(solution)/shard_map/while
  220.9 6.0 %copy-start.4 = (bf16[1536,4,128]{0,2,1:T(8,128)(2,1)S(1)}, bf16[1536,4,128]{0,2,1:T(8,128)(2,1)}, u32[]{:S(2)}) copy-start(bf16[1536,4,128]{0,2,1:T(8,128)(2,1)} %get-tuple-element.294) | copy-start | bytes 4718596 | tf_op jit(solution)/shard_map/while
  231.9 1.0 copy-start.2
  235.8 93.7 %all-to-all-start.3 = ((bf16[8,128,512]{2,1,0:T(8,128)(2,1)}), bf16[8,128,512]{2,1,0:T(8,128)(2,1)S(1)}, u32[]{:S(2)}, u32[]{:S(2)}) async-start(bf16[8,128,512]{2,1,0:T(8,128)(2,1)} %copy.160), calls=%async_computation.3 | async-start | bytes 2097152 | tf_op jit(solution)/shard_map/all_to_all | solution.py:178
  242.0 7.6 %copy-start.3 = (f32[128,8,128]{0,2,1:T(8,128)S(1)}, f32[128,8,128]{0,2,1:T(8,128)}, u32[]{:S(2)}) copy-start(f32[128,8,128]{0,2,1:T(8,128)} %get-tuple-element.214) | copy-start | bytes 1572868
  250.6 36.7 %collective-permute-start.8 = (f32[128,1024]{1,0:T(8,128)}, f32[128,1024]{1,0:T(8,128)}, u32[]{:S(2)}, u32[]{:S(2)}) collective-permute-start(f32[128,1024]{1,0:T(8,128)} %copy.136), channel_id=1, source_target_pairs={{1,0},{2,1},{3,2},{4,3},{5,4},{6,5},{7,6},{9,8},{10,9},{11,10},{12... | collective-permute-start | bytes 1572872 | tf_op jit(solution)/shard_map/ppermute | solution.py:12
  261.8 43.3 %collective-permute-start.13 = (f32[128,1024]{1,0:T(8,128)}, f32[128,1024]{1,0:T(8,128)}, u32[]{:S(2)}, u32[]{:S(2)}) collective-permute-start(f32[128,1024]{1,0:T(8,128)} %copy.145), channel_id=1, source_target_pairs={{2,0},{3,1},{4,2},{5,3},{6,4},{7,5},{10,8},{11,9},{12,10},{13,11},... | collective-permute-start | bytes 1572872 | tf_op jit(solution)/shard_map/ppermute | solution.py:12
  264.1 51.8 %collective-permute-start.14 = (f32[128,1024]{1,0:T(8,128)}, f32[128,1024]{1,0:T(8,128)}, u32[]{:S(2)}, u32[]{:S(2)}) collective-permute-start(f32[128,1024]{1,0:T(8,128)} %copy.146), channel_id=1, source_target_pairs={{3,0},{4,1},{5,2},{6,3},{7,4},{11,8},{12,9},{13,10},{14,11},{15,12... | collective-permute-start | bytes 1572872 | tf_op jit(solution)/shard_map/ppermute | solution.py:12
  266.1 55.4 %collective-permute-start.15 = (f32[128,1024]{1,0:T(8,128)}, f32[128,1024]{1,0:T(8,128)}, u32[]{:S(2)}, u32[]{:S(2)}) collective-permute-start(f32[128,1024]{1,0:T(8,128)} %copy.147), channel_id=1, source_target_pairs={{4,0},{5,1},{6,2},{7,3},{12,8},{13,9},{14,10},{15,11},{20,16},{21,... | collective-permute-start | bytes 1572872 | tf_op jit(solution)/shard_map/ppermute | solution.py:12
  268.2 59.0 %collective-permute-start.12 = (f32[128,1024]{1,0:T(8,128)}, f32[128,1024]{1,0:T(8,128)}, u32[]{:S(2)}, u32[]{:S(2)}) collective-permute-start(f32[128,1024]{1,0:T(8,128)} %copy.143), channel_id=1, source_target_pairs={{1,0},{2,1},{3,2},{4,3},{5,4},{6,5},{7,6},{9,8},{10,9},{11,10},{12... | collective-permute-start | bytes 1572872 | tf_op jit(solution)/shard_map/ppermute | solution.py:12
where the time goes:
time: 336 us; the launch traced here: 332 us
  matrix products  66.5 us (20%)
  starting transfers between devices  64 us (19%)
  blocking collectives  60 us (18%)
  waiting for transfers between devices  60 us (18%)
  local copies, waits for them, and re-layouts  58.1 us (17%)
  other arithmetic  21.1 us (6%)
    psum x1, blocking collectives, body(): flag_total = lax.psum(jnp.sum(flags.astype(jnp.float32)), ('fsdp', 'seq'))  60 us
    ppermute x16, waiting for transfers between devices, passed_along(): return lax.ppermute(block, axis, route)  60 us
    ppermute x16, starting transfers between devices, passed_along(): return lax.ppermute(block, axis, route)  33.5 us
    dot_general x1, matrix products, backward_local(): jnp.einsum('jgqk,qjgd->kjd', d_scores, grouped_q, preferred_element_type=...  16.4 us
    unnamed x26, local copies, waits for them, and re-layouts  15.8 us
    dot_general x1, matrix products, backward_local(): jnp.einsum('jgqk,kjd->qjgd', d_scores, k_window, preferred_element_type=j...  15.3 us
    all_to_all x1, starting transfers between devices, body(): lax.all_to_all(q_next, 'seq', split_axis=1, concat_axis=0, tiled=True)  12 us
    sub x2, other arithmetic, masked_probs(): expo_vals = jnp.exp(scores - row_max)  12 us
  transfers between devices with their start and end apart: 20, of which 5 were waited for; matrix products, arithmetic and copies ran while one was open for 42% of the time, Pallas kernels for 0%

commit v1 on v0

v1 whole, which is shorter than its diff:
```python
import functools
import math

import jax
import jax.numpy as jnp
from jax import lax
from jax.experimental import pallas as pl
from jax.experimental.pallas import tpu as pltpu
from jax.sharding import PartitionSpec as P

HEAD_DIM = 128
SEG_MOST = 512
NT = (((1,), (1,)), ((), ()))


def dot_nt(a, b):
    return lax.dot_general(a, b, NT, preferred_element_type=jnp.float32)


def dot_nn(a, b):
    return jnp.dot(a, b, preferred_element_type=jnp.float32)


def stack_heads(array):
    group = array.shape[1] // HEAD_DIM
    return jnp.concatenate(
        [array[:, g * HEAD_DIM : (g + 1) * HEAD_DIM] for g in range(group)], axis=0
    )


def weights_t(k_win, q_all, bias, group):
    factor = HEAD_DIM ** (-0.5) * math.log2(math.e)
    scores = dot_nt(k_win, q_all) * factor + jnp.concatenate([bias] * group, axis=1)
    top = jnp.max(scores, axis=0, keepdims=True)
    expo = jnp.exp2(scores - top)
    return expo, jnp.sum(expo, axis=0, keepdims=True)


def forward_kernel(blocks, bias_ref, q_ref, *refs):
    k_refs, v_refs, out_ref = refs[:blocks], refs[blocks : 2 * blocks], refs[2 * blocks]
    rows = q_ref.shape[0]
    group = q_ref.shape[1] // HEAD_DIM
    k_win = jnp.concatenate([r[...] for r in k_refs], axis=0)
    v_win = jnp.concatenate([r[...] for r in v_refs], axis=0)
    q_all = stack_heads(q_ref[...])
    expo, total = weights_t(k_win, q_all, bias_ref[...], group)
    out_t = dot_nn(v_win.T, expo.astype(jnp.bfloat16)) * (1.0 / total)
    for g in range(group):
        out_ref[:, g * HEAD_DIM : (g + 1) * HEAD_DIM] = (
            out_t[:, g * rows : (g + 1) * rows].T.astype(out_ref.dtype)
        )


def backward_kernel(blocks, bias_ref, weight_ref, q_ref, up_ref, *refs):
    k_refs, v_refs = refs[:blocks], refs[blocks : 2 * blocks]
    dq_ref = refs[2 * blocks]
    dk_refs = refs[2 * blocks + 1 : 3 * blocks + 1]
    dv_refs = refs[3 * blocks + 1 :]
    rows = q_ref.shape[0]
    group = q_ref.shape[1] // HEAD_DIM
    k_win = jnp.concatenate([r[...] for r in k_refs], axis=0)
    v_win = jnp.concatenate([r[...] for r in v_refs], axis=0)
    q_all = stack_heads(q_ref[...])
    cot = (up_ref[...].astype(jnp.float32) * weight_ref[...]).astype(jnp.bfloat16)
    d_all = stack_heads(cot)
    expo, total = weights_t(k_win, q_all, bias_ref[...], group)
    probs = expo * (1.0 / total)
    d_probs = dot_nt(v_win, d_all)
    delta = jnp.sum(probs * d_probs, axis=0, keepdims=True)
    d_scores = (probs * (d_probs - delta) * (HEAD_DIM ** (-0.5))).astype(jnp.bfloat16)
    dv = dot_nn(probs.astype(jnp.bfloat16), d_all)
    dk = dot_nn(d_scores, q_all)
    for b in range(blocks):
        dk_refs[b][...] = dk[b * rows : (b + 1) * rows].astype(dk_refs[b].dtype)
        dv_refs[b][...] = dv[b * rows : (b + 1) * rows].astype(dv_refs[b].dtype)
    dq_t = dot_nn(k_win.T, d_scores)
    for g in range(group):
        dq_ref[:, g * HEAD_DIM : (g + 1) * HEAD_DIM] = (
            dq_t[:, g * rows : (g + 1) * rows].T.astype(dq_ref.dtype)
        )


def attend(kernel, name, bias, columns, wide, k_blocks, v_blocks, grads, dots):
    blocks = len(k_blocks)
    rows, width = k_blocks[0].shape
    kv_heads = width // HEAD_DIM
    group_width = wide[0].shape[1] // kv_heads

    def whole(array):
        return pl.BlockSpec(array.shape, lambda j: (0, 0))

    narrow_spec = pl.BlockSpec((rows, HEAD_DIM), lambda j: (0, j))
    wide_spec = pl.BlockSpec((rows, group_width), lambda j: (0, j))
    wide_shape = jax.ShapeDtypeStruct(wide[0].shape, jnp.bfloat16)
    narrow_shape = jax.ShapeDtypeStruct((rows, width), jnp.bfloat16)
    flops = dots * 2 * rows * wide[0].shape[1] * blocks * rows
    moved = 2 * rows * ((len(wide) + 1) * wide[0].shape[1] + (2 + grads) * blocks * width)
    return pl.pallas_call(
        functools.partial(kernel, blocks),
        grid=(kv_heads,),
        in_specs=[whole(bias)]
        + [whole(c) for c in columns]
        + [wide_spec] * len(wide)
        + [narrow_spec] * (2 * blocks),
        out_specs=[wide_spec] + [narrow_spec] * (grads * blocks),
        out_shape=[wide_shape] + [narrow_shape] * (grads * blocks),
        compiler_params=pltpu.CompilerParams(
            dimension_semantics=("arbitrary",), vmem_limit_bytes=48 * 1024 * 1024
        ),
        cost_estimate=pl.CostEstimate(
            flops=2 * flops,
            bytes_accessed=moved,
            transcendentals=rows * wide[0].shape[1] * blocks,
        ),
        name=name,
    )(bias, *columns, *wide, *k_blocks, *v_blocks)


def shifted(arrays, distance):
    size = lax.axis_size("seq")
    route = [(i, i + distance) for i in range(size) if 0 <= i + distance < size]
    return [lax.ppermute(a, "seq", route) for a in arrays]


def swapped(arrays):
    size = lax.axis_size("seq")
    route = [(i, i ^ 1) for i in range(size) if (i ^ 1) < size]
    return [lax.ppermute(a, "seq", route) for a in arrays]


def pick(pred, one, other):
    return [jnp.where(pred, a, b) for a, b in zip(one, other)]


def after(arrays, others):
    held = lax.optimization_barrier((tuple(arrays), tuple(others)))
    return list(held[0])


def gather_window(local, hops, is_even):
    got = {0: local}
    for h in range(2, hops + 2, 2):
        got[h] = shifted(got[h - 2], 2)
    for h in range(1, hops + 1, 2):
        got[h] = swapped(pick(is_even, got[h - 1], got[h + 1]))
    return got


def return_sums(parts, hops, is_even):
    came = {h: swapped(parts[h]) for h in range(1, hops + 1, 2)}
    top = hops + hops % 2

    def joined(h):
        terms = [p.astype(jnp.float32) for p in parts[h]] if h in parts else None
        low = came.get(h - 1)
        high = came.get(h + 1)
        if low is None:
            extra = [jnp.where(is_even, b, jnp.zeros_like(b)) for b in high]
        elif high is None:
            extra = [jnp.where(is_even, jnp.zeros_like(a), a) for a in low]
        else:
            extra = pick(is_even, high, low)
        if terms is None:
            return [e.astype(jnp.float32) for e in extra]
        return [t + e.astype(jnp.float32) for t, e in zip(terms, extra)]

    running = joined(top)
    for h in range(top - 2, -1, -2):
        back = shifted([r.astype(jnp.bfloat16) for r in running], -2)
        running = [t + b.astype(jnp.float32) for t, b in zip(joined(h), back)]
    return [r.astype(jnp.bfloat16) for r in running]


def total_over(value, axes):
    for axis in axes:
        size = lax.axis_size(axis)
        if size & (size - 1):
            value = lax.psum(value, axis)
            continue
        step = 1
        while step < size:
            value = value + lax.ppermute(value, axis, [(i, i ^ step) for i in range(size)])
            step *= 2
    return value


def window_bias(seq_ids, rows, hops):
    first = lax.axis_index("seq") * rows
    width = (hops + 1) * rows
    padded = jnp.concatenate([jnp.full((hops * rows,), -1, jnp.int32), seq_ids])
    k_seg = lax.dynamic_slice_in_dim(padded, first, width)
    q_seg = lax.dynamic_slice_in_dim(seq_ids, first, rows)
    k_pos = lax.broadcasted_iota(jnp.int32, (width, rows), 0) - hops * rows
    q_pos = lax.broadcasted_iota(jnp.int32, (width, rows), 1)
    keep = (k_seg[:, None] == q_seg[None, :]) & (k_pos <= q_pos)
    return jnp.where(keep, 0.0, -1e30).astype(jnp.float32)


def body(q_next, k_next, v_next, seg_next, q_prev, k_prev, v_prev, seg_prev, upstream, flags):
    rows = q_next.shape[0]
    seq_size = lax.axis_size("seq")
    token_total = rows * lax.axis_size("fsdp") * seq_size
    hops = min((min(SEG_MOST, rows * seq_size) - 2) // rows + 1, seq_size - 1)
    is_even = lax.axis_index("seq") % 2 == 0
    order = range(hops, -1, -1)

    prev = gather_window([k_prev, v_prev], hops, is_even)
    last = hops + hops % 2
    local_next = after([k_next, v_next], prev[last])
    nxt = gather_window(local_next, hops, is_even)

    flag_total = total_over(jnp.sum(flags.astype(jnp.float32)).reshape(1, 1), ("seq", "fsdp"))
    weight = flags.reshape(rows, 1).astype(jnp.float32) * (
        token_total / jnp.maximum(flag_total, 1.0)
    )
    results = attend(
        backward_kernel,
        "backward",
        window_bias(seg_prev[0], rows, hops),
        [weight],
        [q_prev, upstream],
        [prev[h][0] for h in order],
        [prev[h][1] for h in order],
        2,
        5,
    )
    grad_q = results[0]
    blocks = hops + 1
    parts = {
        h: [results[1 + blocks - 1 - h], results[1 + 2 * blocks - 1 - h]]
        for h in range(blocks)
    }
    grad_k, grad_v = return_sums(parts, hops, is_even)
    (attn_next,) = attend(
        forward_kernel,
        "forward",
        window_bias(seg_next[0], rows, hops),
        [],
        [q_next],
        [nxt[h][0] for h in order],
        [nxt[h][1] for h in order],
        0,
        2,
    )
    return (attn_next, grad_q, grad_k, grad_v)


def solution(mesh):
    tokens = P(("fsdp", "seq"), None)
    ids = P("fsdp", None)
    return jax.shard_map(
        body,
        mesh=mesh,
        in_specs=(
            tokens,
            tokens,
            tokens,
            ids,
            tokens,
            tokens,
            tokens,
            ids,
            tokens,
            P("fsdp", "seq"),
        ),
        out_specs=(tokens, tokens, tokens, tokens),
        check_vma=False,
    )
```

time: 336 us -> 112 us (0.33)
  the two profiles are of different devices: /device:TPU:22 before, /device:TPU:0 now
where the time goes in v1:
time: 112 us; the launch traced here: 111 us
  starting transfers between devices  51.6 us (46%)
  Pallas kernels  23.9 us (21%)
  waiting for transfers between devices  23.2 us (21%)
  other arithmetic  6.5 us (6%)
  between operations  4.77 us (4%)
  local copies, waits for them, and re-layouts  1.57 us (1%)
    ppermute x12, starting transfers between devices, shifted(): return [lax.ppermute(a, 'seq', route) for a in arrays]  34.9 us
    pallas_call x2, Pallas kernels, attend(): pl.pallas_call(functools.partial(kernel, blocks), grid=(kv_heads,), in_sp...  23.9 us
    ppermute x12, waiting for transfers between devices, shifted(): return [lax.ppermute(a, 'seq', route) for a in arrays]  20.7 us
    ppermute x5, starting transfers between devices, total_over(): lax.ppermute(value, axis, [(i, i ^ step) for i in range(size)])  14 us
    select_n x4, other arithmetic, pick(): return [jnp.where(pred, a, b) for a, b in zip(one, other)]  2.71 us
    ppermute x12, starting transfers between devices, swapped(): return [lax.ppermute(a, 'seq', route) for a in arrays]  2.7 us
    ppermute x5, waiting for transfers between devices, total_over(): lax.ppermute(value, axis, [(i, i ^ step) for i in range(size)])  2.46 us
  transfers between devices with their start and end apart: 29, of which 14 were waited for; matrix products, arithmetic and copies ran while one was open for 5% of the time, Pallas kernels for 21%

profile of v1, /device:TPU:0, one launch (start us, length us, event | category | flops | bytes accessed | tf_op | source)
XLA Modules:
  0.0 111.5 jit_solution(16556020573015990840)
XLA Ops:
  0.6 5.0 %collective-permute-start = (bf16[128,1024]{1,0:T(8,128)(2,1)}, bf16[128,1024]{1,0:T(8,128)(2,1)S(1)}, u32[]{:S(2)}, u32[]{:S(2)}) collective-permute-start(bf16[128,1024]{1,0:T(8,128)(2,1)} %refs_4_.2), channel_id=1, source_target_pairs={{0,2},{1,3},{2,4},{3,5},{4,6},{5,7},{8,10},{9,11},{10,12},{11,13},... | collective-permute-start | bytes 786440 | tf_op jit(solution)/shard_map/ppermute | solution.py:122
  5.6 3.5 %collective-permute-start.2 = (bf16[128,1024]{1,0:T(8,128)(2,1)}, bf16[128,1024]{1,0:T(8,128)(2,1)S(1)}, u32[]{:S(2)}, u32[]{:S(2)}) collective-permute-start(bf16[128,1024]{1,0:T(8,128)(2,1)} %refs_9_.2), channel_id=1, source_target_pairs={{0,2},{1,3},{2,4},{3,5},{4,6},{5,7},{8,10},{9,11},{10,12},{11,13},... | collective-permute-start | bytes 786440 | tf_op jit(solution)/shard_map/ppermute | solution.py:122
  9.1 1.3 %convert_reduce_fusion = f32[]{:T(128)} fusion(s32[1,128]{1,0:T(1,128)} %param.19), kind=kLoop, calls=%fused_computation.23 | loop fusion | flops 255 | bytes 516 | tf_op jit(solution)/shard_map/reduce_sum | solution.py:212
  10.4 2.2 %collective-permute-done.refs_2_ = bf16[128,1024]{1,0:T(8,128)(2,1)S(1)} collective-permute-done((bf16[128,1024]{1,0:T(8,128)(2,1)}, bf16[128,1024]{1,0:T(8,128)(2,1)S(1)}, u32[]{:S(2)}, u32[]{:S(2)}) %collective-permute-start) | collective-permute-done | bytes 262176 | tf_op jit(solution)/shard_map/ppermute | solution.py:122
  12.6 4.3 %collective-permute-start.1 = (bf16[128,1024]{1,0:T(8,128)(2,1)S(1)}, bf16[128,1024]{1,0:T(8,128)(2,1)S(1)}, u32[]{:S(2)}, u32[]{:S(2)}) collective-permute-start(bf16[128,1024]{1,0:T(8,128)(2,1)S(1)} %collective-permute-done.refs_2_), channel_id=1, source_target_pairs={{0,2},{1,3},{2,4},{3,5},{4,6},{5,7},{8,10},{9,11},{10,12},{11,13},... | collective-permute-start | bytes 786440 | tf_op jit(solution)/shard_map/ppermute | solution.py:122
  16.9 0.0 copy-start.6
  16.9 0.0 copy-start.5
  16.9 0.7 copy-done.6
  17.6 0.0 copy-done.5
  17.6 0.1 pad_dynamic-slice_fusion
  17.7 0.5 collective-permute-done.2.refs_7_
  18.2 4.3 %collective-permute-start.3 = (bf16[128,1024]{1,0:T(8,128)(2,1)S(1)}, bf16[128,1024]{1,0:T(8,128)(2,1)S(1)}, u32[]{:S(2)}, u32[]{:S(2)}) collective-permute-start(bf16[128,1024]{1,0:T(8,128)(2,1)S(1)} %collective-permute-done.2.refs_7_), channel_id=1, source_target_pairs={{0,2},{1,3},{2,4},{3,5},{4,6},{5,7},{8,10},{9,11},{10,12},{11,13},... | collective-permute-start | bytes 786440 | tf_op jit(solution)/shard_map/ppermute | solution.py:122
  22.5 0.0 copy-start.1
  22.5 1.2 %collective-permute-done.1.refs_0_ = bf16[128,1024]{1,0:T(8,128)(2,1)S(1)} collective-permute-done((bf16[128,1024]{1,0:T(8,128)(2,1)S(1)}, bf16[128,1024]{1,0:T(8,128)(2,1)S(1)}, u32[]{:S(2)}, u32[]{:S(2)}) %collective-permute-start.1) | collective-permute-done | bytes 262176 | tf_op jit(solution)/shard_map/ppermute | solution.py:122
  23.7 1.8 %broadcast_select_fusion.2 = (bf16[128,1024]{1,0:T(8,128)(2,1)}, bf16[128,1024]{1,0:T(8,128)(2,1)}) fusion(bf16[128,1024]{1,0:T(8,128)(2,1)} %refs_4_.2, bf16[128,1024]{1,0:T(8,128)(2,1)S(1)} %collective-permute-done.refs_2_, pred[]{:T(512)S(6)} %eq.39, bf16[128,1024]{1,0:T(8,128)(2,1)S(1)} %collective-permute-done.1.refs_0_), kind=kLoop, calls=%fused_computation.13 | loop fusion | flops 262144 | bytes 1310721 | tf_op jit(solution)/shard_map/jit(_where)/select_n | solution.py:132
  25.5 0.0 collective-permute-start.17
  25.5 0.5 collective-permute-start.18
  26.0 2.2 %collective-permute-done.3.refs_5_ = bf16[128,1024]{1,0:T(8,128)(2,1)S(1)} collective-permute-done((bf16[128,1024]{1,0:T(8,128)(2,1)S(1)}, bf16[128,1024]{1,0:T(8,128)(2,1)S(1)}, u32[]{:S(2)}, u32[]{:S(2)}) %collective-permute-start.3) | collective-permute-done | bytes 262176 | tf_op jit(solution)/shard_map/ppermute | solution.py:122
  28.2 0.8 broadcast_select_fusion
  29.0 0.5 collective-permute-start.20
  29.6 0.3 fusion.3
  31.1 3.8 %collective-permute-start.13 = (f32[1,1]{1,0:T(1,128)}, f32[1,1]{1,0:T(1,128)}, u32[]{:S(2)}, u32[]{:S(2)}) collective-permute-start(f32[1,1]{1,0:T(1,128)} %add.66), channel_id=1, source_target_pairs={{0,2},{1,3},{2,0},{3,1},{4,6},{5,7},{6,4},{7,5},{8,10},{9,11},{10,... | collective-permute-start | bytes 20 | tf_op jit(solution)/shard_map/ppermute | solution.py:182
  34.9 0.4 collective-permute-done.13
  35.9 4.4 %collective-permute-start.14 = (f32[1,1]{1,0:T(1,128)}, f32[1,1]{1,0:T(1,128)}, u32[]{:S(2)}, u32[]{:S(2)}) collective-permute-start(f32[1,1]{1,0:T(1,128)} %add.67), channel_id=1, source_target_pairs={{0,4},{1,5},{2,6},{3,7},{4,0},{5,1},{6,2},{7,3},{8,12},{9,13},{10,... | collective-permute-start | bytes 20 | tf_op jit(solution)/shard_map/ppermute | solution.py:182
  40.3 0.4 collective-permute-done.14
  41.3 2.9 %collective-permute-start.15 = (f32[1,1]{1,0:T(1,128)}, f32[1,1]{1,0:T(1,128)}, u32[]{:S(2)}, u32[]{:S(2)}) collective-permute-start(f32[1,1]{1,0:T(1,128)} %add.68), channel_id=1, source_target_pairs={{0,8},{8,0},{16,24},{24,16},{1,9},{9,1},{17,25},{25,17},{2,10},{10... | collective-permute-start | bytes 20 | tf_op jit(solution)/shard_map/ppermute | solution.py:182
  44.2 0.9 collective-permute-done.15
  45.7 2.9 %collective-permute-start.16 = (f32[1,1]{1,0:T(1,128)}, f32[1,1]{1,0:T(1,128)}, u32[]{:S(2)}, u32[]{:S(2)}) collective-permute-start(f32[1,1]{1,0:T(1,128)} %add.69), channel_id=1, source_target_pairs={{0,16},{8,24},{16,0},{24,8},{1,17},{9,25},{17,1},{25,9},{2,18},{10... | collective-permute-start | bytes 20 | tf_op jit(solution)/shard_map/ppermute | solution.py:182
  48.6 0.9 collective-permute-done.16
  50.1 0.0 copy-start.7
  50.1 0.6 copy-done.7
  50.8 0.1 copy.14.weight_ref
  50.9 3.8 %collective-permute-start.8 = (bf16[128,1024]{1,0:T(8,128)(2,1)S(1)}, bf16[128,1024]{1,0:T(8,128)(2,1)S(1)}, u32[]{:S(2)}, u32[]{:S(2)}) collective-permute-start(bf16[128,1024]{1,0:T(8,128)(2,1)S(1)} %copy-done.3), channel_id=1, source_target_pairs={{0,2},{1,3},{2,4},{3,5},{4,6},{5,7},{8,10},{9,11},{10,12},{11,13},... | collective-permute-start | bytes 786440 | tf_op jit(solution)/shard_map/ppermute | solution.py:122
  54.7 0.0 collective-permute-done.17.refs_1_
  54.8 3.5 %collective-permute-start.4 = (bf16[128,1024]{1,0:T(8,128)(2,1)S(1)}, bf16[128,1024]{1,0:T(8,128)(2,1)S(1)}, u32[]{:S(2)}, u32[]{:S(2)}) collective-permute-start(bf16[128,1024]{1,0:T(8,128)(2,1)S(1)} %copy-done.2), channel_id=1, source_target_pairs={{0,2},{1,3},{2,4},{3,5},{4,6},{5,7},{8,10},{9,11},{10,12},{11,13},... | collective-permute-start | bytes 786440 | tf_op jit(solution)/shard_map/ppermute | solution.py:122
  58.3 0.0 collective-permute-done.18.refs_3_
  58.3 0.0 collective-permute-done.19.refs_6_
  58.3 15.7 %backward.1 = (bf16[128,4096]{1,0:T(8,128)(2,1)}, bf16[128,1024]{1,0:T(8,128)(2,1)S(1)}, bf16[128,1024]{1,0:T(8,128)(2,1)S(1)}, bf16[128,1024]{1,0:T(8,128)(2,1)...) custom-call(f32[640,128]{1,0:T(8,128)S(1)} %get-tuple-element.38.bia, ...), custom_call_target="tpu_custom_call" | custom-call | flops 6710886400 | bytes 8388608 | tf_op jit(solution)/shard_map/backward/pallas_call | solution.py:98
  74.0 0.5 collective-permute-start.22
  74.6 0.0 collective-permute-done.8.refs_7_
  74.6 0.5 collective-permute-start.21
  75.1 0.0 collective-permute-done.4.refs_2_
  75.1 3.5 %collective-permute-start.9 = (bf16[128,1024]{1,0:T(8,128)(2,1)S(1)}, bf16[128,1024]{1,0:T(8,128)(2,1)S(1)}, u32[]{:S(2)}, u32[]{:S(2)}) collective-permute-start(bf16[128,1024]{1,0:T(8,128)(2,1)S(1)} %collective-permute-done.8.refs_7_), channel_id=1, source_target_pairs={{0,2},{1,3},{2,4},{3,5},{4,6},{5,7},{8,10},{9,11},{10,12},{11,13},... | collective-permute-start | bytes 786440 | tf_op jit(solution)/shard_map/ppermute | solution.py:122
  78.5 0.0 collective-permute-done.26
  78.6 1.9 %collective-permute-start.5 = (bf16[128,1024]{1,0:T(8,128)(2,1)S(1)}, bf16[128,1024]{1,0:T(8,128)(2,1)S(1)}, u32[]{:S(2)}, u32[]{:S(2)}) collective-permute-start(bf16[128,1024]{1,0:T(8,128)(2,1)S(1)} %collective-permute-done.4.refs_2_), channel_id=1, source_target_pairs={{0,2},{1,3},{2,4},{3,5},{4,6},{5,7},{8,10},{9,11},{10,12},{11,13},... | collective-permute-start | bytes 786440 | tf_op jit(solution)/shard_map/ppermute | solution.py:122
  80.5 0.1 add_convert_fusion.2
  80.6 1.3 %collective-permute-start.27 = (bf16[128,1024]{1,0:T(8,128)(2,1)S(1)}, bf16[128,1024]{1,0:T(8,128)(2,1)S(1)}, u32[]{:S(2)}, u32[]{:S(2)}) collective-permute-start(bf16[128,1024]{1,0:T(8,128)(2,1)S(1)} %add_convert_fusion.2), channel_id=1, source_target_pairs={{2,0},{3,1},{4,2},{5,3},{6,4},{7,5},{10,8},{11,9},{12,10},{13,11},... | collective-permute-start | bytes 786440 | tf_op jit(solution)/shard_map/ppermute | solution.py:122
  81.9 0.1 add_convert_fusion.5
  82.0 3.2 %collective-permute-done.9.refs_5_ = bf16[128,1024]{1,0:T(8,128)(2,1)S(1)} collective-permute-done((bf16[128,1024]{1,0:T(8,128)(2,1)S(1)}, bf16[128,1024]{1,0:T(8,128)(2,1)S(1)}, u32[]{:S(2)}, u32[]{:S(2)}) %collective-permute-start.9) | collective-permute-done | bytes 262176 | tf_op jit(solution)/shard_map/ppermute | solution.py:122
  85.2 1.3 %collective-permute-start.23 = (bf16[128,1024]{1,0:T(8,128)(2,1)S(1)}, bf16[128,1024]{1,0:T(8,128)(2,1)S(1)}, u32[]{:S(2)}, u32[]{:S(2)}) collective-permute-start(bf16[128,1024]{1,0:T(8,128)(2,1)S(1)} %add_convert_fusion.5), channel_id=1, source_target_pairs={{2,0},{3,1},{4,2},{5,3},{6,4},{7,5},{10,8},{11,9},{12,10},{13,11},... | collective-permute-start | bytes 786440 | tf_op jit(solution)/shard_map/ppermute | solution.py:122
  86.6 3.3 %collective-permute-done.5.refs_0_ = bf16[128,1024]{1,0:T(8,128)(2,1)S(1)} collective-permute-done((bf16[128,1024]{1,0:T(8,128)(2,1)S(1)}, bf16[128,1024]{1,0:T(8,128)(2,1)S(1)}, u32[]{:S(2)}, u32[]{:S(2)}) %collective-permute-start.5) | collective-permute-done | bytes 262176 | tf_op jit(solution)/shard_map/ppermute | solution.py:122
  89.9 0.6 collective-permute-start.11
  90.5 0.1 collective-permute-start.6
  90.6 1.1 collective-permute-done.27
  91.7 0.2 add_convert_fusion.1
  91.8 4.2 %collective-permute-done.23 = bf16[128,1024]{1,0:T(8,128)(2,1)S(1)} collective-permute-done((bf16[128,1024]{1,0:T(8,128)(2,1)S(1)}, bf16[128,1024]{1,0:T(8,128)(2,1)S(1)}, u32[]{:S(2)}, u32[]{:S(2)}) %collective-permute-start.23) | collective-permute-done | bytes 262176 | tf_op jit(solution)/shard_map/ppermute | solution.py:122
  96.0 1.3 %collective-permute-start.28 = (bf16[128,1024]{1,0:T(8,128)(2,1)S(1)}, bf16[128,1024]{1,0:T(8,128)(2,1)S(1)}, u32[]{:S(2)}, u32[]{:S(2)}) collective-permute-start(bf16[128,1024]{1,0:T(8,128)(2,1)S(1)} %add_convert_fusion.1), channel_id=1, source_target_pairs={{2,0},{3,1},{4,2},{5,3},{6,4},{7,5},{10,8},{11,9},{12,10},{13,11},... | collective-permute-start | bytes 786440 | tf_op jit(solution)/shard_map/ppermute | solution.py:122
  97.3 0.2 add_convert_fusion.4
  97.5 1.3 %collective-permute-start.24 = (bf16[128,1024]{1,0:T(8,128)(2,1)S(1)}, bf16[128,1024]{1,0:T(8,128)(2,1)S(1)}, u32[]{:S(2)}, u32[]{:S(2)}) collective-permute-start(bf16[128,1024]{1,0:T(8,128)(2,1)S(1)} %add_convert_fusion.4), channel_id=1, source_target_pairs={{2,0},{3,1},{4,2},{5,3},{6,4},{7,5},{10,8},{11,9},{12,10},{13,11},... | collective-permute-start | bytes 786440 | tf_op jit(solution)/shard_map/ppermute | solution.py:122
  98.9 8.2 %forward.1 = bf16[128,4096]{1,0:T(8,128)(2,1)} custom-call(f32[640,128]{1,0:T(8,128)S(1)} %get-tuple-element.39.bias_ref, bf16[128,4096]{1,0:T(8,128)(2,1)S(1)} %copy-done.4, bf16[128,1024]{1,0:T(8,128)(2,1)S(1)} %collective-permute-done.5.refs_0_, bf16[128,1024]{1,0:T(8,128)(2,1)S(1)} %collective-permute-done.6.refs_1_, ...), custom_call_target="tpu_custom_call" | custom-call | flops 2684354560 | bytes 4718592 | tf_op jit(solution)/shard_map/forward/pallas_call | solution.py:98
  107.0 0.1 collective-permute-done.28
  107.1 0.8 add_convert_fusion
  107.9 2.7 %collective-permute-done.24 = bf16[128,1024]{1,0:T(8,128)(2,1)S(1)} collective-permute-done((bf16[128,1024]{1,0:T(8,128)(2,1)S(1)}, bf16[128,1024]{1,0:T(8,128)(2,1)S(1)}, u32[]{:S(2)}, u32[]{:S(2)}) %collective-permute-start.24) | collective-permute-done | bytes 262176 | tf_op jit(solution)/shard_map/ppermute | solution.py:122
  110.6 0.8 add_convert_fusion.3
  (29 shorter events, 0.2 us)
Async XLA Ops:
  0.6 12.0 %collective-permute-start = (bf16[128,1024]{1,0:T(8,128)(2,1)}, bf16[128,1024]{1,0:T(8,128)(2,1)S(1)}, u32[]{:S(2)}, u32[]{:S(2)}) collective-permute-start(bf16[128,1024]{1,0:T(8,128)(2,1)} %refs_4_.2), channel_id=1, source_target_pairs={{0,2},{1,3},{2,4},{3,5},{4,6},{5,7},{8,10},{9,11},{10,12},{11,13},... | collective-permute-start | bytes 786440 | tf_op jit(solution)/shard_map/ppermute | solution.py:122
  5.6 12.6 %collective-permute-start.2 = (bf16[128,1024]{1,0:T(8,128)(2,1)}, bf16[128,1024]{1,0:T(8,128)(2,1)S(1)}, u32[]{:S(2)}, u32[]{:S(2)}) collective-permute-start(bf16[128,1024]{1,0:T(8,128)(2,1)} %refs_9_.2), channel_id=1, source_target_pairs={{0,2},{1,3},{2,4},{3,5},{4,6},{5,7},{8,10},{9,11},{10,12},{11,13},... | collective-permute-start | bytes 786440 | tf_op jit(solution)/shard_map/ppermute | solution.py:122
  10.4 19.5 %collective-permute-start.12 = (f32[1,1]{1,0:T(1,128)}, f32[1,1]{1,0:T(1,128)}, u32[]{:S(2)}, u32[]{:S(2)}) collective-permute-start(f32[1,1]{1,0:T(1,128)} %bitcast.4), channel_id=1, source_target_pairs={{0,1},{1,0},{2,3},{3,2},{4,5},{5,4},{6,7},{7,6},{8,9},{9,8},{10,11... | collective-permute-start | bytes 20 | tf_op jit(solution)/shard_map/ppermute | solution.py:182
  12.6 11.1 %collective-permute-start.1 = (bf16[128,1024]{1,0:T(8,128)(2,1)S(1)}, bf16[128,1024]{1,0:T(8,128)(2,1)S(1)}, u32[]{:S(2)}, u32[]{:S(2)}) collective-permute-start(bf16[128,1024]{1,0:T(8,128)(2,1)S(1)} %collective-permute-done.refs_2_), channel_id=1, source_target_pairs={{0,2},{1,3},{2,4},{3,5},{4,6},{5,7},{8,10},{9,11},{10,12},{11,13},... | collective-permute-start | bytes 786440 | tf_op jit(solution)/shard_map/ppermute | solution.py:122
  16.9 0.7 copy-start.6
  16.9 0.7 copy-start.5
  18.2 10.0 %collective-permute-start.3 = (bf16[128,1024]{1,0:T(8,128)(2,1)S(1)}, bf16[128,1024]{1,0:T(8,128)(2,1)S(1)}, u32[]{:S(2)}, u32[]{:S(2)}) collective-permute-start(bf16[128,1024]{1,0:T(8,128)(2,1)S(1)} %collective-permute-done.2.refs_7_), channel_id=1, source_target_pairs={{0,2},{1,3},{2,4},{3,5},{4,6},{5,7},{8,10},{9,11},{10,12},{11,13},... | collective-permute-start | bytes 786440 | tf_op jit(solution)/shard_map/ppermute | solution.py:122
  22.5 5.7 %copy-start.1 = (bf16[128,1024]{1,0:T(8,128)(2,1)S(1)}, bf16[128,1024]{1,0:T(8,128)(2,1)}, u32[]{:S(2)}) copy-start(bf16[128,1024]{1,0:T(8,128)(2,1)} %refs_9_.2) | copy-start | bytes 786436
  25.5 29.2 %collective-permute-start.17 = (bf16[128,1024]{1,0:T(8,128)(2,1)}, bf16[128,1024]{1,0:T(8,128)(2,1)S(1)}, u32[]{:S(2)}, u32[]{:S(2)}) collective-permute-start(bf16[128,1024]{1,0:T(8,128)(2,1)} %get-tuple-element.33), channel_id=1, source_target_pairs={{0,1},{1,0},{2,3},{3,2},{4,5},{5,4},{6,7},{7,6},{8,9},{9,8},{10,11... | collective-permute-start | bytes 786440 | tf_op jit(solution)/shard_map/ppermute | solution.py:128
  25.5 32.7 %collective-permute-start.18 = (bf16[128,1024]{1,0:T(8,128)(2,1)}, bf16[128,1024]{1,0:T(8,128)(2,1)S(1)}, u32[]{:S(2)}, u32[]{:S(2)}) collective-permute-start(bf16[128,1024]{1,0:T(8,128)(2,1)} %get-tuple-element.32), channel_id=1, source_target_pairs={{0,1},{1,0},{2,3},{3,2},{4,5},{5,4},{6,7},{7,6},{8,9},{9,8},{10,11... | collective-permute-start | bytes 786440 | tf_op jit(solution)/shard_map/ppermute | solution.py:128
  28.2 22.7 %copy-start.3 = (bf16[128,1024]{1,0:T(8,128)(2,1)S(1)}, bf16[128,1024]{1,0:T(8,128)(2,1)}, u32[]{:S(2)}) copy-start(bf16[128,1024]{1,0:T(8,128)(2,1)} %refs_9_.1) | copy-start | bytes 786436
  29.0 29.2 %collective-permute-start.19 = (bf16[128,1024]{1,0:T(8,128)(2,1)}, bf16[128,1024]{1,0:T(8,128)(2,1)}, u32[]{:S(2)}, u32[]{:S(2)}) collective-permute-start(bf16[128,1024]{1,0:T(8,128)(2,1)} %get-tuple-element.31), channel_id=1, source_target_pairs={{0,1},{1,0},{2,3},{3,2},{4,5},{5,4},{6,7},{7,6},{8,9},{9,8},{10,11... | collective-permute-start | bytes 786440 | tf_op jit(solution)/shard_map/ppermute | solution.py:128
  29.0 29.2 %collective-permute-start.20 = (bf16[128,1024]{1,0:T(8,128)(2,1)}, bf16[128,1024]{1,0:T(8,128)(2,1)}, u32[]{:S(2)}, u32[]{:S(2)}) collective-permute-start(bf16[128,1024]{1,0:T(8,128)(2,1)} %get-tuple-element.30), channel_id=1, source_target_pairs={{0,1},{1,0},{2,3},{3,2},{4,5},{5,4},{6,7},{7,6},{8,9},{9,8},{10,11... | collective-permute-start | bytes 786440 | tf_op jit(solution)/shard_map/ppermute | solution.py:128
  29.6 25.2 %copy-start.2 = (bf16[128,1024]{1,0:T(8,128)(2,1)S(1)}, bf16[128,1024]{1,0:T(8,128)(2,1)}, u32[]{:S(2)}) copy-start(bf16[128,1024]{1,0:T(8,128)(2,1)} %refs_4_.1) | copy-start | bytes 786436
  29.6 28.7 %copy-start = (bf16[128,1024]{1,0:T(8,128)(2,1)S(1)}, bf16[128,1024]{1,0:T(8,128)(2,1)}, u32[]{:S(2)}) copy-start(bf16[128,1024]{1,0:T(8,128)(2,1)} %refs_4_.2) | copy-start | bytes 786436
  31.1 4.2 %collective-permute-start.13 = (f32[1,1]{1,0:T(1,128)}, f32[1,1]{1,0:T(1,128)}, u32[]{:S(2)}, u32[]{:S(2)}) collective-permute-start(f32[1,1]{1,0:T(1,128)} %add.66), channel_id=1, source_target_pairs={{0,2},{1,3},{2,0},{3,1},{4,6},{5,7},{6,4},{7,5},{8,10},{9,11},{10,... | collective-permute-start | bytes 20 | tf_op jit(solution)/shard_map/ppermute | solution.py:182
  35.9 4.8 %collective-permute-start.14 = (f32[1,1]{1,0:T(1,128)}, f32[1,1]{1,0:T(1,128)}, u32[]{:S(2)}, u32[]{:S(2)}) collective-permute-start(f32[1,1]{1,0:T(1,128)} %add.67), channel_id=1, source_target_pairs={{0,4},{1,5},{2,6},{3,7},{4,0},{5,1},{6,2},{7,3},{8,12},{9,13},{10,... | collective-permute-start | bytes 20 | tf_op jit(solution)/shard_map/ppermute | solution.py:182
  41.3 3.7 %collective-permute-start.15 = (f32[1,1]{1,0:T(1,128)}, f32[1,1]{1,0:T(1,128)}, u32[]{:S(2)}, u32[]{:S(2)}) collective-permute-start(f32[1,1]{1,0:T(1,128)} %add.68), channel_id=1, source_target_pairs={{0,8},{8,0},{16,24},{24,16},{1,9},{9,1},{17,25},{25,17},{2,10},{10... | collective-permute-start | bytes 20 | tf_op jit(solution)/shard_map/ppermute | solution.py:182
  45.7 3.7 %collective-permute-start.16 = (f32[1,1]{1,0:T(1,128)}, f32[1,1]{1,0:T(1,128)}, u32[]{:S(2)}, u32[]{:S(2)}) collective-permute-start(f32[1,1]{1,0:T(1,128)} %add.69), channel_id=1, source_target_pairs={{0,16},{8,24},{16,0},{24,8},{1,17},{9,25},{17,1},{25,9},{2,18},{10... | collective-permute-start | bytes 20 | tf_op jit(solution)/shard_map/ppermute | solution.py:182
  50.1 0.7 copy-start.7
  50.9 23.7 %collective-permute-start.8 = (bf16[128,1024]{1,0:T(8,128)(2,1)S(1)}, bf16[128,1024]{1,0:T(8,128)(2,1)S(1)}, u32[]{:S(2)}, u32[]{:S(2)}) collective-permute-start(bf16[128,1024]{1,0:T(8,128)(2,1)S(1)} %copy-done.3), channel_id=1, source_target_pairs={{0,2},{1,3},{2,4},{3,5},{4,6},{5,7},{8,10},{9,11},{10,12},{11,13},... | collective-permute-start | bytes 786440 | tf_op jit(solution)/shard_map/ppermute | solution.py:122
  54.8 20.3 %collective-permute-start.4 = (bf16[128,1024]{1,0:T(8,128)(2,1)S(1)}, bf16[128,1024]{1,0:T(8,128)(2,1)S(1)}, u32[]{:S(2)}, u32[]{:S(2)}) collective-permute-start(bf16[128,1024]{1,0:T(8,128)(2,1)S(1)} %copy-done.2), channel_id=1, source_target_pairs={{0,2},{1,3},{2,4},{3,5},{4,6},{5,7},{8,10},{9,11},{10,12},{11,13},... | collective-permute-start | bytes 786440 | tf_op jit(solution)/shard_map/ppermute | solution.py:122
  74.0 4.5 %collective-permute-start.26 = (bf16[128,1024]{1,0:T(8,128)(2,1)S(1)}, bf16[128,1024]{1,0:T(8,128)(2,1)S(1)}, u32[]{:S(2)}, u32[]{:S(2)}) collective-permute-start(bf16[128,1024]{1,0:T(8,128)(2,1)S(1)} %get-tuple-element.28), channel_id=1, source_target_pairs={{0,1},{1,0},{2,3},{3,2},{4,5},{5,4},{6,7},{7,6},{8,9},{9,8},{10,11... | collective-permute-start | bytes 786440 | tf_op jit(solution)/shard_map/ppermute | solution.py:128
  74.0 6.5 %collective-permute-start.22 = (bf16[128,1024]{1,0:T(8,128)(2,1)S(1)}, bf16[128,1024]{1,0:T(8,128)(2,1)S(1)}, u32[]{:S(2)}, u32[]{:S(2)}) collective-permute-start(bf16[128,1024]{1,0:T(8,128)(2,1)S(1)} %get-tuple-element.23), channel_id=1, source_target_pairs={{0,1},{1,0},{2,3},{3,2},{4,5},{5,4},{6,7},{7,6},{8,9},{9,8},{10,11... | collective-permute-start | bytes 786440 | tf_op jit(solution)/shard_map/ppermute | solution.py:128
  74.6 15.4 %collective-permute-start.25 = (bf16[128,1024]{1,0:T(8,128)(2,1)S(1)}, bf16[128,1024]{1,0:T(8,128)(2,1)S(1)}, u32[]{:S(2)}, u32[]{:S(2)}) collective-permute-start(bf16[128,1024]{1,0:T(8,128)(2,1)S(1)} %get-tuple-element.26), channel_id=1, source_target_pairs={{0,1},{1,0},{2,3},{3,2},{4,5},{5,4},{6,7},{7,6},{8,9},{9,8},{10,11... | collective-permute-start | bytes 786440 | tf_op jit(solution)/shard_map/ppermute | solution.py:128
  74.6 16.0 %collective-permute-start.21 = (bf16[128,1024]{1,0:T(8,128)(2,1)S(1)}, bf16[128,1024]{1,0:T(8,128)(2,1)S(1)}, u32[]{:S(2)}, u32[]{:S(2)}) collective-permute-start(bf16[128,1024]{1,0:T(8,128)(2,1)S(1)} %get-tuple-element.21), channel_id=1, source_target_pairs={{0,1},{1,0},{2,3},{3,2},{4,5},{5,4},{6,7},{7,6},{8,9},{9,8},{10,11... | collective-permute-start | bytes 786440 | tf_op jit(solution)/shard_map/ppermute | solution.py:128
  75.1 10.1 %collective-permute-start.9 = (bf16[128,1024]{1,0:T(8,128)(2,1)S(1)}, bf16[128,1024]{1,0:T(8,128)(2,1)S(1)}, u32[]{:S(2)}, u32[]{:S(2)}) collective-permute-start(bf16[128,1024]{1,0:T(8,128)(2,1)S(1)} %collective-permute-done.8.refs_7_), channel_id=1, source_target_pairs={{0,2},{1,3},{2,4},{3,5},{4,6},{5,7},{8,10},{9,11},{10,12},{11,13},... | collective-permute-start | bytes 786440 | tf_op jit(solution)/shard_map/ppermute | solution.py:122
  78.6 11.3 %collective-permute-start.5 = (bf16[128,1024]{1,0:T(8,128)(2,1)S(1)}, bf16[128,1024]{1,0:T(8,128)(2,1)S(1)}, u32[]{:S(2)}, u32[]{:S(2)}) collective-permute-start(bf16[128,1024]{1,0:T(8,128)(2,1)S(1)} %collective-permute-done.4.refs_2_), channel_id=1, source_target_pairs={{0,2},{1,3},{2,4},{3,5},{4,6},{5,7},{8,10},{9,11},{10,12},{11,13},... | collective-permute-start | bytes 786440 | tf_op jit(solution)/shard_map/ppermute | solution.py:122
  80.6 11.1 %collective-permute-start.27 = (bf16[128,1024]{1,0:T(8,128)(2,1)S(1)}, bf16[128,1024]{1,0:T(8,128)(2,1)S(1)}, u32[]{:S(2)}, u32[]{:S(2)}) collective-permute-start(bf16[128,1024]{1,0:T(8,128)(2,1)S(1)} %add_convert_fusion.2), channel_id=1, source_target_pairs={{2,0},{3,1},{4,2},{5,3},{6,4},{7,5},{10,8},{11,9},{12,10},{13,11},... | collective-permute-start | bytes 786440 | tf_op jit(solution)/shard_map/ppermute | solution.py:122
  85.2 10.8 %collective-permute-start.23 = (bf16[128,1024]{1,0:T(8,128)(2,1)S(1)}, bf16[128,1024]{1,0:T(8,128)(2,1)S(1)}, u32[]{:S(2)}, u32[]{:S(2)}) collective-permute-start(bf16[128,1024]{1,0:T(8,128)(2,1)S(1)} %add_convert_fusion.5), channel_id=1, source_target_pairs={{2,0},{3,1},{4,2},{5,3},{6,4},{7,5},{10,8},{11,9},{12,10},{13,11},... | collective-permute-start | bytes 786440 | tf_op jit(solution)/shard_map/ppermute | solution.py:122
  89.9 7.6 %collective-permute-start.10 = (bf16[128,1024]{1,0:T(8,128)(2,1)S(1)}, bf16[128,1024]{1,0:T(8,128)(2,1)S(1)}, u32[]{:S(2)}, u32[]{:S(2)}) collective-permute-start(bf16[128,1024]{1,0:T(8,128)(2,1)S(1)} %get-tuple-element.35), channel_id=1, source_target_pairs={{0,1},{1,0},{2,3},{3,2},{4,5},{5,4},{6,7},{7,6},{8,9},{9,8},{10,11... | collective-permute-start | bytes 786440 | tf_op jit(solution)/shard_map/ppermute | solution.py:128
  89.9 8.9 %collective-permute-start.11 = (bf16[128,1024]{1,0:T(8,128)(2,1)S(1)}, bf16[128,1024]{1,0:T(8,128)(2,1)S(1)}, u32[]{:S(2)}, u32[]{:S(2)}) collective-permute-start(bf16[128,1024]{1,0:T(8,128)(2,1)S(1)} %get-tuple-element.34), channel_id=1, source_target_pairs={{0,1},{1,0},{2,3},{3,2},{4,5},{5,4},{6,7},{7,6},{8,9},{9,8},{10,11... | collective-permute-start | bytes 786440 | tf_op jit(solution)/shard_map/ppermute | solution.py:128
  90.5 8.3 %collective-permute-start.6 = (bf16[128,1024]{1,0:T(8,128)(2,1)S(1)}, bf16[128,1024]{1,0:T(8,128)(2,1)S(1)}, u32[]{:S(2)}, u32[]{:S(2)}) collective-permute-start(bf16[128,1024]{1,0:T(8,128)(2,1)S(1)} %get-tuple-element.37), channel_id=1, source_target_pairs={{0,1},{1,0},{2,3},{3,2},{4,5},{5,4},{6,7},{7,6},{8,9},{9,8},{10,11... | collective-permute-start | bytes 786440 | tf_op jit(solution)/shard_map/ppermute | solution.py:128
  91.7 7.2 %collective-permute-start.7 = (bf16[128,1024]{1,0:T(8,128)(2,1)S(1)}, bf16[128,1024]{1,0:T(8,128)(2,1)S(1)}, u32[]{:S(2)}, u32[]{:S(2)}) collective-permute-start(bf16[128,1024]{1,0:T(8,128)(2,1)S(1)} %get-tuple-element.36), channel_id=1, source_target_pairs={{0,1},{1,0},{2,3},{3,2},{4,5},{5,4},{6,7},{7,6},{8,9},{9,8},{10,11... | collective-permute-start | bytes 786440 | tf_op jit(solution)/shard_map/ppermute | solution.py:128
  91.7 7.2 %copy-start.4 = (bf16[128,4096]{1,0:T(8,128)(2,1)S(1)}, bf16[128,4096]{1,0:T(8,128)(2,1)}, u32[]{:S(2)}) copy-start(bf16[128,4096]{1,0:T(8,128)(2,1)} %q_ref.2) | copy-start | bytes 3145732
  96.0 11.1 %collective-permute-start.28 = (bf16[128,1024]{1,0:T(8,128)(2,1)S(1)}, bf16[128,1024]{1,0:T(8,128)(2,1)S(1)}, u32[]{:S(2)}, u32[]{:S(2)}) collective-permute-start(bf16[128,1024]{1,0:T(8,128)(2,1)S(1)} %add_convert_fusion.1), channel_id=1, source_target_pairs={{2,0},{3,1},{4,2},{5,3},{6,4},{7,5},{10,8},{11,9},{12,10},{13,11},... | collective-permute-start | bytes 786440 | tf_op jit(solution)/shard_map/ppermute | solution.py:122
  97.5 13.1 %collective-permute-start.24 = (bf16[128,1024]{1,0:T(8,128)(2,1)S(1)}, bf16[128,1024]{1,0:T(8,128)(2,1)S(1)}, u32[]{:S(2)}, u32[]{:S(2)}) collective-permute-start(bf16[128,1024]{1,0:T(8,128)(2,1)S(1)} %add_convert_fusion.4), channel_id=1, source_target_pairs={{2,0},{3,1},{4,2},{5,3},{6,4},{7,5},{10,8},{11,9},{12,10},{13,11},... | collective-permute-start | bytes 786440 | tf_op jit(solution)/shard_map/ppermute | solution.py:122

commit v2 on v1

v2 whole, which is shorter than its diff:
```python
import functools
import math

import jax
import jax.numpy as jnp
from jax import lax
from jax.experimental import pallas as pl
from jax.experimental.pallas import tpu as pltpu
from jax.sharding import PartitionSpec as P

HEAD_DIM = 128
SEG_MOST = 512
NT = (((1,), (1,)), ((), ()))
MESH = pl.DeviceIdType.MESH


def dot_nt(a, b):
    return lax.dot_general(a, b, NT, preferred_element_type=jnp.float32)


def dot_nn(a, b):
    return jnp.dot(a, b, preferred_element_type=jnp.float32)


def stack_heads(array):
    group = array.shape[1] // HEAD_DIM
    return jnp.concatenate(
        [array[:, g * HEAD_DIM : (g + 1) * HEAD_DIM] for g in range(group)], axis=0
    )


def weights_t(k_win, q_all, bias, group):
    factor = HEAD_DIM ** (-0.5) * math.log2(math.e)
    scores = dot_nt(k_win, q_all) * factor + jnp.concatenate([bias] * group, axis=1)
    top = jnp.max(scores, axis=0, keepdims=True)
    expo = jnp.exp2(scores - top)
    return expo, jnp.sum(expo, axis=0, keepdims=True)


def down_rows(row, rows):
    return jnp.broadcast_to(row.astype(jnp.float32), (rows, rows)).T


def kernel(
    hops,
    sizes,
    q_next,
    k_next,
    v_next,
    seg_next,
    q_prev,
    k_prev,
    v_prev,
    seg_prev,
    upstream,
    flags,
    attn_out,
    dq_out,
    dk_out,
    dv_out,
    window,
    bias,
    weight,
    grads,
    grad_in,
    sums,
    sums_in,
    count,
    count_in,
    local_sem,
    send_sem,
    recv_sem,
    grad_send,
    grad_recv,
    count_send,
    count_recv,
):
    fsdp_size, seq_size = sizes
    rows = q_next.shape[0]
    kv_heads = k_next.shape[1] // HEAD_DIM
    wide = q_next.shape[1] // kv_heads
    group = wide // HEAD_DIM
    top = hops + hops % 2
    me = lax.axis_index("seq")
    row_of = lax.axis_index("fsdp")
    parity = lax.rem(me, 2)
    partner = me + 1 - 2 * parity
    has_after = me + 2 < seq_size
    has_before = me >= 2

    def flipped(value, step):
        return value + step - 2 * step * lax.rem(value // step, 2)

    count_to = []
    greet = []
    for axis, size in (("fsdp", fsdp_size), ("seq", seq_size)):
        step = 1
        while step < size:
            if axis == "seq":
                count_to.append((row_of, flipped(me, step)))
            else:
                count_to.append((flipped(row_of, step), me))
            if (axis, step) != ("seq", 2):
                greet.append(count_to[-1])
            step *= 2

    barrier = pltpu.get_barrier_semaphore()

    @pl.when(has_after)
    def _():
        pl.semaphore_signal(barrier, inc=1, device_id=(row_of, me + 2), device_id_type=MESH)

    @pl.when(has_before)
    def _():
        pl.semaphore_signal(barrier, inc=1, device_id=(row_of, me - 2), device_id_type=MESH)

    for target in greet:
        pl.semaphore_signal(barrier, inc=1, device_id=target, device_id_type=MESH)

    def own(m, part, j):
        source = ((k_prev, v_prev), (k_next, v_next))[m][part]
        return pltpu.make_async_copy(
            source.at[:, pl.ds(pl.multiple_of(j * HEAD_DIM, HEAD_DIM), HEAD_DIM)],
            window.at[m, 0, j, pl.ds(part * rows, rows)],
            local_sem.at[m, part, j],
        )

    for m in range(2):

        @pl.loop(0, kv_heads)
        def _(j, m=m):
            own(m, 0, j).start()
            own(m, 1, j).start()

    neighbours = jnp.where(has_after, 1, 0) + jnp.where(has_before, 1, 0)
    pl.semaphore_wait(barrier, len(greet) + neighbours)

    def hop(m, o, j):
        return pltpu.make_async_remote_copy(
            src_ref=window.at[m, o - 2, j],
            dst_ref=window.at[m, o, j],
            send_sem=send_sem.at[m, o, j],
            recv_sem=recv_sem.at[m, o, j],
            device_id=(row_of, me + 2),
            device_id_type=MESH,
        )

    def swap(m, o, j):
        return pltpu.make_async_remote_copy(
            src_ref=window.at[m, o - 1 + 2 * parity, j],
            dst_ref=window.at[m, o, j],
            send_sem=send_sem.at[m, o, j],
            recv_sem=recv_sem.at[m, o, j],
            device_id=(row_of, partner),
            device_id_type=MESH,
        )

    def swap_start(m, o, j, by):
        @pl.when((parity == by) & (partner >= o))
        def _():
            swap(m, o, j).start()

    def start_hop(m, o, j):
        @pl.when(has_after & (me >= o - 2))
        def _():
            hop(m, o, j).start()

    def arrive_hop(m, o, j):
        @pl.when(me >= o)
        def _():
            hop(m, o, j).wait_recv()

    def arrive_swap(m, o, j):
        @pl.when(me >= o)
        def _():
            swap(m, o, j).wait_recv()

    def first_hops(m):
        @pl.loop(0, kv_heads)
        def _(j):
            own(m, 0, j).wait()
            own(m, 1, j).wait()
            start_hop(m, 2, j)

    def on_hop(m, o, j):
        arrive_hop(m, o, j)
        if o + 2 <= top:
            start_hop(m, o + 2, j)
        if o - 1 <= hops:
            if o == 2:
                swap_start(m, 1, j, 0)
            swap_start(m, o - 1, j, 1)
        if o + 1 <= hops:
            swap_start(m, o + 1, j, 0)

    first_hops(0)

    here = jnp.sum(flags[...].astype(jnp.float32), axis=1, keepdims=True)
    count[0] = jnp.broadcast_to(here, count.shape[1:])
    for s, target in enumerate(count_to):
        copy = pltpu.make_async_remote_copy(
            src_ref=count.at[s],
            dst_ref=count_in.at[s],
            send_sem=count_send.at[s],
            recv_sem=count_recv.at[s],
            device_id=target,
            device_id_type=MESH,
        )
        copy.start()
        if s == 0:
            for o in range(1, top + 1):

                @pl.when(me < o)
                def _(o=o):
                    for m in range(2):

                        @pl.loop(0, kv_heads)
                        def _(j):
                            window[m, o, j] = jnp.zeros(window.shape[3:], window.dtype)

            @pl.when(jnp.logical_not(has_after))
            def _():
                for part in range(top // 2):

                    @pl.loop(0, kv_heads)
                    def _(j):
                        sums_in[part, j] = jnp.zeros(sums_in.shape[2:], sums_in.dtype)

            for m, seg in ((0, seg_prev), (1, seg_next)):
                q_seg = seg[:, pl.ds(pl.multiple_of(me * rows, rows), rows)].astype(jnp.float32)
                k_at = lax.broadcasted_iota(jnp.int32, (rows, rows), 0)
                q_at = lax.broadcasted_iota(jnp.int32, (rows, rows), 1)
                for o in range(hops + 1):
                    block = jnp.maximum(me - o, 0)
                    k_seg = seg[:, pl.ds(pl.multiple_of(block * rows, rows), rows)]
                    keep = (down_rows(k_seg, rows) == q_seg) & (k_at - o * rows <= q_at)
                    gone = jnp.where(me >= o, 0.0, -1e30)
                    bias[m, pl.ds(o * rows, rows)] = jnp.where(keep, gone, -1e30)
        copy.wait()
        count[s + 1] = count[s] + count_in[s]
    token_total = float(rows * fsdp_size * seq_size)
    scale = token_total / jnp.maximum(count[len(count_to)][:1], 1.0)
    weight[...] = down_rows(flags[...], rows) * scale[:, :1]

    @pl.loop(0, kv_heads)
    def _(j):
        on_hop(0, 2, j)

    first_hops(1)

    def blocks_of(m, part, j):
        return jnp.concatenate(
            [window[m, o, j, part * rows : (part + 1) * rows] for o in range(hops + 1)], axis=0
        )

    def columns(j):
        return pl.ds(pl.multiple_of(j * wide, wide), wide)

    def backward(j):
        k_win = blocks_of(0, 0, j)
        v_win = blocks_of(0, 1, j)
        q_all = stack_heads(q_prev[:, columns(j)])
        up_all = stack_heads(upstream[:, columns(j)]).astype(jnp.float32)
        d_all = (up_all * jnp.concatenate([weight[...]] * group, axis=0)).astype(jnp.bfloat16)
        expo, total = weights_t(k_win, q_all, bias[0], group)
        probs = expo * (1.0 / total)
        d_probs = dot_nt(v_win, d_all)
        delta = jnp.sum(probs * d_probs, axis=0, keepdims=True)
        d_scores = (probs * (d_probs - delta) * (HEAD_DIM ** (-0.5))).astype(jnp.bfloat16)
        dv = dot_nn(probs.astype(jnp.bfloat16), d_all).astype(jnp.bfloat16)
        dk = dot_nn(d_scores, q_all).astype(jnp.bfloat16)
        for o in range(hops + 1):
            grads[o, j, :rows] = dk[o * rows : (o + 1) * rows]
            grads[o, j, rows:] = dv[o * rows : (o + 1) * rows]
        dq_t = dot_nn(k_win.T, d_scores)
        dq_out[:, columns(j)] = jnp.concatenate(
            [dq_t[:, g * rows : (g + 1) * rows].T for g in range(group)], axis=1
        ).astype(dq_out.dtype)

    def forward(j):
        k_win = blocks_of(1, 0, j)
        v_win = blocks_of(1, 1, j)
        q_all = stack_heads(q_next[:, columns(j)])
        expo, total = weights_t(k_win, q_all, bias[1], group)
        out_t = dot_nn(v_win.T, expo.astype(jnp.bfloat16)) * (1.0 / total)
        attn_out[:, columns(j)] = jnp.concatenate(
            [out_t[:, g * rows : (g + 1) * rows].T for g in range(group)], axis=1
        ).astype(attn_out.dtype)

    def later_hops(m, j):
        for o in range(4, top + 1, 2):
            on_hop(m, o, j)

    def grad_swap(o, j):
        return pltpu.make_async_remote_copy(
            src_ref=grads.at[o, j],
            dst_ref=grad_in.at[o // 2, j],
            send_sem=grad_send.at[o, j],
            recv_sem=grad_recv.at[o, j],
            device_id=(row_of, partner),
            device_id_type=MESH,
        )

    def sum_back(o, j):
        return pltpu.make_async_remote_copy(
            src_ref=sums.at[o // 2 - 1, j],
            dst_ref=sums_in.at[o // 2 - 1, j],
            send_sem=grad_send.at[o, j],
            recv_sem=grad_recv.at[o, j],
            device_id=(row_of, me - 2),
            device_id_type=MESH,
        )

    def joined(o, j):
        even = jnp.where(parity == 0, 1.0, 0.0)
        acc = jnp.zeros(grads.shape[2:], jnp.float32)
        if o <= hops:
            acc = grads[o, j].astype(jnp.float32)
        if o + 1 <= hops:
            acc = acc + grad_in[o // 2, j].astype(jnp.float32) * even
        if o > 0:
            acc = acc + grad_in[o // 2 - 1, j].astype(jnp.float32) * (1.0 - even)
        if o + 2 <= top:
            acc = acc + sums_in[o // 2, j].astype(jnp.float32)
        return acc

    def send_sum(o, j):
        sums[o // 2 - 1, j] = joined(o, j).astype(sums.dtype)

        @pl.when(has_before)
        def _():
            sum_back(o, j).start()

    def arrive_sum(o, j):
        @pl.when(has_after)
        def _():
            sum_back(o, j).wait_recv()

    def first_sum(j):
        for o in range(1, hops + 1, 2):
            grad_swap(o, j).wait_recv()
        send_sum(top, j)

    def ready(m, j):
        for o in range(1, hops + 1, 2):
            arrive_swap(m, o, j)

    later_hops(0, 0)

    @pl.loop(0, kv_heads)
    def _(j):
        @pl.when(j + 1 < kv_heads)
        def _():
            later_hops(0, j + 1)

        ready(0, j)
        backward(j)
        for o in range(1, hops + 1, 2):
            grad_swap(o, j).start()

        @pl.when(j > 0)
        def _():
            first_sum(j - 1)

    first_sum(kv_heads - 1)

    @pl.loop(0, kv_heads)
    def _(j):
        on_hop(1, 2, j)
        for o in range(top - 2, 0, -2):
            arrive_sum(o + 2, j)
            send_sum(o, j)

    later_hops(1, 0)

    @pl.loop(0, kv_heads)
    def _(j):
        @pl.when(j + 1 < kv_heads)
        def _():
            later_hops(1, j + 1)

        ready(1, j)
        forward(j)

    @pl.loop(0, kv_heads)
    def _(j):
        arrive_sum(2, j)
        acc = joined(0, j).astype(jnp.bfloat16)
        spot = pl.ds(pl.multiple_of(j * HEAD_DIM, HEAD_DIM), HEAD_DIM)
        dk_out[:, spot] = acc[:rows]
        dv_out[:, spot] = acc[rows:]

    @pl.loop(0, kv_heads)
    def _(j):
        for m in range(2):
            for o in range(2, top + 1, 2):

                @pl.when(has_after & (me >= o - 2))
                def _(m=m, o=o):
                    hop(m, o, j).wait_send()

            for o in range(1, hops + 1, 2):

                @pl.when(partner >= o)
                def _(m=m, o=o):
                    swap(m, o, j).wait_send()

        for o in range(1, hops + 1, 2):
            grad_swap(o, j).wait_send()
        for o in range(2, top + 1, 2):

            @pl.when(has_before)
            def _(o=o):
                sum_back(o, j).wait_send()


def make_body(fsdp_size, seq_size):
    def body(q_next, k_next, v_next, seg_next, q_prev, k_prev, v_prev, seg_prev, upstream, flags):
        rows, width = k_next.shape
        kv_heads = width // HEAD_DIM
        hops = min((min(SEG_MOST, rows * seq_size) - 2) // rows + 1, seq_size - 1)
        top = hops + hops % 2
        steps = fsdp_size.bit_length() + seq_size.bit_length() - 2
        piece = (2 * rows, HEAD_DIM)
        near = pl.BlockSpec(memory_space=pltpu.VMEM)
        far = pl.BlockSpec(memory_space=pl.ANY)
        call = pl.pallas_call(
            functools.partial(kernel, hops, (fsdp_size, seq_size)),
            in_specs=[near, far, far, near, near, far, far, near, near, near],
            out_specs=[near] * 4,
            out_shape=[
                jax.ShapeDtypeStruct(q_next.shape, jnp.bfloat16),
                jax.ShapeDtypeStruct(q_prev.shape, jnp.bfloat16),
                jax.ShapeDtypeStruct(k_prev.shape, jnp.bfloat16),
                jax.ShapeDtypeStruct(v_prev.shape, jnp.bfloat16),
            ],
            scratch_shapes=[
                pltpu.VMEM((2, top + 1, kv_heads) + piece, jnp.bfloat16),
                pltpu.VMEM((2, (hops + 1) * rows, rows), jnp.float32),
                pltpu.VMEM((rows, rows), jnp.float32),
                pltpu.VMEM((hops + 1, kv_heads) + piece, jnp.bfloat16),
                pltpu.VMEM(((hops + 1) // 2, kv_heads) + piece, jnp.bfloat16),
                pltpu.VMEM((top // 2, kv_heads) + piece, jnp.bfloat16),
                pltpu.VMEM((top // 2, kv_heads) + piece, jnp.bfloat16),
                pltpu.VMEM((steps + 1, 8, 128), jnp.float32),
                pltpu.VMEM((steps, 8, 128), jnp.float32),
                pltpu.SemaphoreType.DMA((2, 2, kv_heads)),
                pltpu.SemaphoreType.DMA((2, top + 1, kv_heads)),
                pltpu.SemaphoreType.DMA((2, top + 1, kv_heads)),
                pltpu.SemaphoreType.DMA((top + 1, kv_heads)),
                pltpu.SemaphoreType.DMA((top + 1, kv_heads)),
                pltpu.SemaphoreType.DMA((steps,)),
                pltpu.SemaphoreType.DMA((steps,)),
            ],
            compiler_params=pltpu.CompilerParams(
                collective_id=0, has_side_effects=True, vmem_limit_bytes=60 * 1024 * 1024
            ),
            name="attention_pair",
        )
        return tuple(
            call(
                q_next,
                k_next,
                v_next,
                seg_next,
                q_prev,
                k_prev,
                v_prev,
                seg_prev,
                upstream,
                flags,
            )
        )

    return body


def solution(mesh):
    tokens = P(("fsdp", "seq"), None)
    ids = P("fsdp", None)
    return jax.shard_map(
        make_body(mesh.shape["fsdp"], mesh.shape["seq"]),
        mesh=mesh,
        in_specs=(
            tokens,
            tokens,
            tokens,
            ids,
            tokens,
            tokens,
            tokens,
            ids,
            tokens,
            P("fsdp", "seq"),
        ),
        out_specs=(tokens, tokens, tokens, tokens),
        check_vma=False,
    )
```

time: 112 us -> 65.7 us (0.59)
  the two profiles are of different devices: /device:TPU:0 before, /device:TPU:22 now
where the time goes in v2:
time: 65.7 us; the launch traced here: 65.5 us
  Pallas kernels  59.6 us (91%)
  local copies, waits for them, and re-layouts  5.22 us (8%)
    pallas_call x1, Pallas kernels, body(): call(q_next, k_next, v_next, seg_next, q_prev, k_prev, v_prev, seg_prev,...  59.6 us
    unnamed x10, local copies, waits for them, and re-layouts  5.22 us

profile of v2, /device:TPU:22, one launch (start us, length us, event | category | flops | bytes accessed | tf_op | source)
XLA Modules:
  0.0 65.5 jit_solution(5068767203438006915)
XLA Ops:
  0.6 59.6 %attention_pair.1 = (bf16[128,4096]{1,0:T(8,128)(2,1)}, bf16[128,4096]{1,0:T(8,128)(2,1)}, bf16[128,1024]{1,0:T(8,128)(2,1)}, bf16[128,1024]{1,0:T(8,128)(2,1)}) custom-call(bf16[128,4096]{1,0:T(8,128)(2,1)} %q_next.1, bf16[128,1024]{1,0:T(8,128)(2,1)} %k_next.1, bf16[128,1024]{1,0:T(8,128)(2,1)} %v_next.1, s32[1,1024]{1,0:T(1,128)} %seg_next.1, ...), custom_call_target="tpu_custom_call" | custom-call | tf_op jit(solution)/shard_map/attention_pair/pallas_call | solution.py:461
  60.2 0.0 copy-start
  60.2 2.4 %copy.18 = bf16[128,4096]{1,0:T(8,128)(2,1)} copy(bf16[128,4096]{1,0:T(8,128)(2,1)} %get-tuple-element.8) | data formatting | bytes 2097152
  62.6 0.0 copy-done
  62.6 0.0 copy-start.2
  62.6 1.0 %copy.19 = bf16[128,4096]{1,0:T(8,128)(2,1)} copy(bf16[128,4096]{1,0:T(8,128)(2,1)S(1)} %copy-done) | data formatting | bytes 2097152
  63.6 0.1 copy-done.2
  63.7 0.0 copy-start.1
  63.7 0.7 %copy.20 = bf16[128,1024]{1,0:T(8,128)(2,1)} copy(bf16[128,1024]{1,0:T(8,128)(2,1)S(1)} %copy-done.2) | data formatting | bytes 524288
  64.4 0.3 copy-done.1
  64.7 0.7 %copy.21 = bf16[128,1024]{1,0:T(8,128)(2,1)} copy(bf16[128,1024]{1,0:T(8,128)(2,1)S(1)} %copy-done.1) | data formatting | bytes 524288
Async XLA Ops:
  60.2 2.4 %copy-start = (bf16[128,4096]{1,0:T(8,128)(2,1)S(1)}, bf16[128,4096]{1,0:T(8,128)(2,1)}, u32[]{:S(2)}) copy-start(bf16[128,4096]{1,0:T(8,128)(2,1)} %get-tuple-element.9) | copy-start | bytes 3145732
  62.6 1.1 %copy-start.2 = (bf16[128,1024]{1,0:T(8,128)(2,1)S(1)}, bf16[128,1024]{1,0:T(8,128)(2,1)}, u32[]{:S(2)}) copy-start(bf16[128,1024]{1,0:T(8,128)(2,1)} %get-tuple-element.10) | copy-start | bytes 786436
  63.7 1.0 %copy-start.1 = (bf16[128,1024]{1,0:T(8,128)(2,1)S(1)}, bf16[128,1024]{1,0:T(8,128)(2,1)}, u32[]{:S(2)}) copy-start(bf16[128,1024]{1,0:T(8,128)(2,1)} %get-tuple-element.11) | copy-start | bytes 786436

commit v3 on v2

--- a/solution.py
+++ b/solution.py
@@ -44,20 +44,24 @@
 def kernel(
     hops,
     sizes,
-    q_next,
+    q_next_far,
     k_next,
     v_next,
     seg_next,
-    q_prev,
+    q_prev_far,
     k_prev,
     v_prev,
     seg_prev,
-    upstream,
+    upstream_far,
     flags,
     attn_out,
     dq_out,
     dk_out,
     dv_out,
+    q_next,
+    q_prev,
+    upstream,
+    wide_sem,
     window,
     bias,
     weight,
@@ -93,8 +97,8 @@
 
     count_to = []
     greet = []
-    for axis, size in (("fsdp", fsdp_size), ("seq", seq_size)):
-        step = 1
+    for axis, low, size in (("seq", 2, seq_size), ("seq", 1, 2), ("fsdp", 1, fsdp_size)):
+        step = low
         while step < size:
             if axis == "seq":
                 count_to.append((row_of, flipped(me, step)))
@@ -132,6 +136,15 @@
             own(m, 0, j).start()
             own(m, 1, j).start()
 
+    wide_copies = [
+        pltpu.make_async_copy(source, target, wide_sem.at[i])
+        for i, (source, target) in enumerate(
+            ((q_prev_far, q_prev), (upstream_far, upstream), (q_next_far, q_next))
+        )
+    ]
+    for copy in wide_copies:
+        copy.start()
+
     neighbours = jnp.where(has_after, 1, 0) + jnp.where(has_before, 1, 0)
     pl.semaphore_wait(barrier, len(greet) + neighbours)
 
@@ -175,8 +188,8 @@
         def _():
             swap(m, o, j).wait_recv()
 
-    def first_hops(m):
-        @pl.loop(0, kv_heads)
+    def first_hops(m, low=0, high=kv_heads):
+        @pl.loop(low, high)
         def _(j):
             own(m, 0, j).wait()
             own(m, 1, j).wait()
@@ -193,10 +206,9 @@
         if o + 1 <= hops:
             swap_start(m, o + 1, j, 0)
 
-    first_hops(0)
-
     here = jnp.sum(flags[...].astype(jnp.float32), axis=1, keepdims=True)
     count[0] = jnp.broadcast_to(here, count.shape[1:])
+    chunk = -(-kv_heads // len(count_to))
     for s, target in enumerate(count_to):
         copy = pltpu.make_async_remote_copy(
             src_ref=count.at[s],
@@ -207,6 +219,8 @@
             device_id_type=MESH,
         )
         copy.start()
+        if s * chunk < kv_heads:
+            first_hops(0, s * chunk, min((s + 1) * chunk, kv_heads))
         if s == 0:
             for o in range(1, top + 1):
 
@@ -345,6 +359,8 @@
         for o in range(1, hops + 1, 2):
             arrive_swap(m, o, j)
 
+    for copy in wide_copies:
+        copy.wait()
     later_hops(0, 0)
 
     @pl.loop(0, kv_heads)
@@ -379,16 +395,13 @@
         def _():
             later_hops(1, j + 1)
 
-        ready(1, j)
-        forward(j)
-
-    @pl.loop(0, kv_heads)
-    def _(j):
         arrive_sum(2, j)
         acc = joined(0, j).astype(jnp.bfloat16)
         spot = pl.ds(pl.multiple_of(j * HEAD_DIM, HEAD_DIM), HEAD_DIM)
         dk_out[:, spot] = acc[:rows]
         dv_out[:, spot] = acc[rows:]
+        ready(1, j)
+        forward(j)
 
     @pl.loop(0, kv_heads)
     def _(j):
@@ -412,6 +425,29 @@
             @pl.when(has_before)
             def _(o=o):
                 sum_back(o, j).wait_send()
+
+
+def place_kernel(*refs):
+    half = len(refs) // 2
+    for source, target in zip(refs[:half], refs[half:]):
+        target[...] = source[...]
+
+
+def placed(parts, arrays):
+    steps = math.gcd(parts, 4)
+    specs = [
+        pl.BlockSpec((a.shape[0], a.shape[1] // steps), lambda j: (0, j)) for a in arrays
+    ]
+    return tuple(
+        pl.pallas_call(
+            place_kernel,
+            grid=(steps,),
+            in_specs=specs,
+            out_specs=specs,
+            out_shape=[jax.ShapeDtypeStruct(a.shape, a.dtype) for a in arrays],
+            name="place",
+        )(*arrays)
+    )
 
 
 def make_body(fsdp_size, seq_size):
@@ -426,7 +462,7 @@
         far = pl.BlockSpec(memory_space=pl.ANY)
         call = pl.pallas_call(
             functools.partial(kernel, hops, (fsdp_size, seq_size)),
-            in_specs=[near, far, far, near, near, far, far, near, near, near],
+            in_specs=[far, far, far, near, far, far, far, near, far, near],
             out_specs=[near] * 4,
             out_shape=[
                 jax.ShapeDtypeStruct(q_next.shape, jnp.bfloat16),
@@ -435,6 +471,10 @@
                 jax.ShapeDtypeStruct(v_prev.shape, jnp.bfloat16),
             ],
             scratch_shapes=[
+                pltpu.VMEM(q_next.shape, jnp.bfloat16),
+                pltpu.VMEM(q_prev.shape, jnp.bfloat16),
+                pltpu.VMEM(upstream.shape, jnp.bfloat16),
+                pltpu.SemaphoreType.DMA((3,)),
                 pltpu.VMEM((2, top + 1, kv_heads) + piece, jnp.bfloat16),
                 pltpu.VMEM((2, (hops + 1) * rows, rows), jnp.float32),
                 pltpu.VMEM((rows, rows), jnp.float32),
@@ -457,7 +497,8 @@
             ),
             name="attention_pair",
         )
-        return tuple(
+        return placed(
+            kv_heads,
             call(
                 q_next,
                 k_next,
@@ -469,7 +510,7 @@
                 seg_prev,
                 upstream,
                 flags,
-            )
+            ),
         )
 
     return body

time: 65.7 us -> 60.9 us (0.927); the launches traced: 65.5 us -> 60 us
  local copies, waits for them, and re-layouts: 5.22 us -> 0 us
    unnamed x10 -> x0, local copies, waits for them, and re-layouts: 5.22 us -> none
    pallas_call x1, Pallas kernels: 59.6 us -> 55.5 us  [body(): call(q_next, k_next, v_next, seg_next, q_prev, k_prev, v_prev, seg_prev,...]
    pallas_call x0 -> x1, Pallas kernels: none -> 3.87 us  [placed(): pl.pallas_call(place_kernel, grid=(steps,), in_specs=specs, out_specs=spe...]
where the time goes in v3:
time: 60.9 us; the launch traced here: 60 us
  Pallas kernels  59.3 us (97%)
  between operations  0.64 us (1%)
    pallas_call x1, Pallas kernels, body(): call(q_next, k_next, v_next, seg_next, q_prev, k_prev, v_prev, seg_prev,...  55.5 us
    pallas_call x1, Pallas kernels, placed(): pl.pallas_call(place_kernel, grid=(steps,), in_specs=specs, out_specs=spe...  3.87 us

profile of v3, /device:TPU:22, one launch (start us, length us, event | category | flops | bytes accessed | tf_op | source)
XLA Modules:
  0.0 60.0 jit_solution(10331089449838338963)
XLA Ops:
  0.6 55.5 %attention_pair.1 = (bf16[128,4096]{1,0:T(8,128)(2,1)}, bf16[128,4096]{1,0:T(8,128)(2,1)}, bf16[128,1024]{1,0:T(8,128)(2,1)}, bf16[128,1024]{1,0:T(8,128)(2,1)}) custom-call(bf16[128,4096]{1,0:T(8,128)(2,1)} %q_next_far.1, bf16[128,1024]{1,0:T(8,128)(2,1)} %k_next.1, bf16[128,1024]{1,0:T(8,128)(2,1)} %v_next.1, s32[1,1024]{1,0:T(1,128)} %seg_next.1, ...), custom_call_target="tpu_custom_call" | custom-call | tf_op jit(solution)/shard_map/attention_pair/pallas_call | solution.py:502
  56.1 3.9 %place.1 = (bf16[128,4096]{1,0:T(8,128)(2,1)}, bf16[128,4096]{1,0:T(8,128)(2,1)}, bf16[128,1024]{1,0:T(8,128)(2,1)}, bf16[128,1024]{1,0:T(8,128)(2,1)}) custom-call(bf16[128,4096]{1,0:T(8,128)(2,1)} %get-tuple-element.8.refs_0_, bf16[128,4096]{1,0:T(8,128)(2,1)} %get-tuple-element.9.refs_1_, bf16[128,1024]{1,0:T(8,128)(2,1)} %get-tuple-element.10.refs_2_, ...), custom_call_target="tpu_custom_call" | custom-call | tf_op jit(solution)/shard_map/place/pallas_call | solution.py:442
